TPU v7x, 256 devices: a whole 4x4x8 slice. The times are simulated.
256 devices in a mesh: ctx: 64 (over x, z, y_lo), head: 4 (over y_hi, core).
Axes of the slice: x: 4, y: 4 (y_hi: 2, y_lo: 2; y = y_hi * 2 + y_lo), z: 8, core: 2. Of those that a mesh axis runs over, the one named last changes fastest.
Arguments:
- queries: bfloat16 [16384, 2048], P('ctx', 'head'), may hold values from -32 to 32
- key_heads: bfloat16 [16384, 2048], P('ctx', 'head'), may hold values from -32 to 32
- value_heads: bfloat16 [16384, 2048], P('ctx', 'head'), may hold values from -6 to 6
- out_weight: bfloat16 [4096, 2048], P('ctx', 'head'), may hold values from -0.5 to 0.5
- block_lists: int32 [128, 3], replicated, may hold values from 0 to 127, as said below
- out_grad: bfloat16 [16384, 4096], P('ctx', 'head'), may hold values from -16 to 16
Outputs:
- attended: bfloat16 [16384, 4096], P('ctx', 'head')
- query_grad: bfloat16 [16384, 2048], P('ctx', 'head')
- key_grad: bfloat16 [16384, 2048], P('ctx', 'head')
- value_grad: bfloat16 [16384, 2048], P('ctx', 'head')
- weight_grad: float32 [4096, 2048], P('ctx', 'head')
Inputs may be any that keep to these rules, and one draw needn't show every extreme that they name: `block_lists`: every entry of row b lies within 4 blocks of b, and the first entry of each row lies exactly 4 blocks away from b.
All inputs are finite; a program needn't handle non-finite values.
Results may differ from a plain program's by a relative error of at most 0.028.
Values may be sent and summed in bfloat16 or wider, within the bound.
A program may use at most 128 MiB of HBM per device.

v0:
```python
import jax
import jax.numpy as jnp
from jax import lax
from jax.sharding import PartitionSpec as P

HD = 128
BLK = 128
CYCLE = 2


def passed_along(x, axis, by):
    peers = lax.axis_size(axis)
    return lax.ppermute(x, axis, [(i, (i + by) % peers) for i in range(peers)])


def spread(value, axis, source):
    kept = jnp.where(lax.axis_index(axis) == source, value, 0).astype(value.dtype)
    return lax.psum(kept, axis)


def local(queries, key_heads, value_heads, out_weight, block_lists, out_grad):
    head_size = HD
    block = BLK
    reach_runs = CYCLE
    scale = head_size ** (-0.5)
    tok_dev = queries.shape[0]
    features = queries.shape[1]
    groups = features // head_size
    per_dev = tok_dev // block
    total_blocks = per_dev * lax.axis_size("ctx")
    run_index = lax.axis_index("ctx")
    band_count = 2 * reach_runs + 1
    stacked = jnp.stack([key_heads, value_heads])
    moving = passed_along(stacked, "ctx", -reach_runs)
    pieces = [moving]
    for turn in range(2 * reach_runs):
        moving = passed_along(moving, "ctx", 1)
        pieces.append(moving)
    pieces = pieces[::-1]
    band = jnp.stack(pieces)
    first = spread(stacked[:, :block], "ctx", 0)
    band_ids = (run_index - reach_runs) * per_dev + jnp.arange(
        band_count * per_dev, dtype=jnp.int32
    )
    query_ids = run_index * per_dev + jnp.arange(per_dev, dtype=jnp.int32)
    local_lists = lax.dynamic_slice_in_dim(block_lists, run_index * per_dev, per_dev, 0)
    listed = jnp.any(local_lists[:, :, None] == band_ids[None, None, :], axis=1)
    nearby = jnp.abs(band_ids[None, :] - query_ids[:, None]) <= 1
    inside = (band_ids >= 1) & (band_ids < total_blocks)
    allowed = (listed | nearby) & inside[None, :]
    token_mask = jnp.repeat(jnp.repeat(allowed, block, 0), block, 1)
    band_keys = band[:, 0].reshape(band_count * tok_dev, groups, head_size)
    band_values = band[:, 1].reshape(band_count * tok_dev, groups, head_size)
    first_keys = first[0].reshape(block, groups, head_size)
    first_values = first[1].reshape(block, groups, head_size)
    query_view = queries.reshape(tok_dev, groups, head_size)
    band_scores = (
        jnp.einsum("qhd,khd->hqk", query_view, band_keys, preferred_element_type=jnp.float32)
        * scale
    )
    first_scores = (
        jnp.einsum("qhd,khd->hqk", query_view, first_keys, preferred_element_type=jnp.float32)
        * scale
    )
    band_scores = jnp.where(token_mask[None], band_scores, -jnp.inf)
    row_top = jnp.maximum(jnp.max(band_scores, axis=2), jnp.max(first_scores, axis=2))
    band_exp = jnp.exp(band_scores - row_top[:, :, None])
    first_exp = jnp.exp(first_scores - row_top[:, :, None])
    denominator = jnp.sum(band_exp, axis=2) + jnp.sum(first_exp, axis=2)
    band_prob = band_exp / denominator[:, :, None]
    first_prob = first_exp / denominator[:, :, None]
    band_low = band_prob.astype(jnp.bfloat16)
    first_low = first_prob.astype(jnp.bfloat16)
    mixed_heads = jnp.einsum(
        "hqk,khd->qhd", band_low, band_values, preferred_element_type=jnp.float32
    )
    mixed_heads = mixed_heads + jnp.einsum(
        "hqk,khd->qhd", first_low, first_values, preferred_element_type=jnp.float32
    )
    mixed = mixed_heads.reshape(tok_dev, features).astype(jnp.bfloat16)
    contract_last = (((1,), (1,)), ((), ()))
    full_weight = lax.all_gather(out_weight, "ctx", axis=0, tiled=True)
    partial_out = lax.dot_general(
        mixed, full_weight, contract_last, preferred_element_type=jnp.float32
    )
    attended = lax.psum_scatter(
        partial_out.astype(jnp.bfloat16), "head", scatter_dimension=1, tiled=True
    )
    grad_full = lax.all_gather(out_grad, "head", axis=1, tiled=True)
    mixed_grad = jnp.dot(grad_full, full_weight, preferred_element_type=jnp.float32)
    mixed_grad = mixed_grad.astype(jnp.bfloat16)
    weight_grad = lax.psum_scatter(
        lax.dot_general(
            grad_full, mixed, (((0,), (0,)), ((), ())), preferred_element_type=jnp.float32
        ),
        "ctx",
        scatter_dimension=0,
        tiled=True,
    )
    grad_view = mixed_grad.reshape(tok_dev, groups, head_size)
    delta = jnp.sum(
        grad_view.astype(jnp.float32)
        * mixed.reshape(tok_dev, groups, head_size).astype(jnp.float32),
        axis=2,
    ).T
    band_dots = jnp.einsum(
        "qhd,khd->hqk", grad_view, band_values, preferred_element_type=jnp.float32
    )
    first_dots = jnp.einsum(
        "qhd,khd->hqk", grad_view, first_values, preferred_element_type=jnp.float32
    )
    band_slopes = (band_prob * (band_dots - delta[:, :, None])).astype(jnp.bfloat16)
    first_slopes = (first_prob * (first_dots - delta[:, :, None])).astype(jnp.bfloat16)
    query_sum = jnp.einsum(
        "hqk,khd->qhd", band_slopes, band_keys, preferred_element_type=jnp.float32
    )
    query_sum = query_sum + jnp.einsum(
        "hqk,khd->qhd", first_slopes, first_keys, preferred_element_type=jnp.float32
    )
    query_grad = (query_sum * scale).reshape(tok_dev, features).astype(jnp.bfloat16)
    band_dk = jnp.einsum(
        "hqk,qhd->khd", band_slopes, query_view, preferred_element_type=jnp.float32
    )
    band_dv = jnp.einsum("hqk,qhd->khd", band_low, grad_view, preferred_element_type=jnp.float32)
    partials = jnp.stack(
        [
            band_dk.reshape(band_count, tok_dev, features),
            band_dv.reshape(band_count, tok_dev, features),
        ],
        axis=1,
    )
    first_dk = jnp.einsum(
        "hqk,qhd->khd", first_slopes, query_view, preferred_element_type=jnp.float32
    )
    first_dv = jnp.einsum("hqk,qhd->khd", first_low, grad_view, preferred_element_type=jnp.float32)
    first_part = jnp.stack([first_dk.reshape(block, features), first_dv.reshape(block, features)])
    carried = partials[0]
    for turn in range(1, 2 * reach_runs + 1):
        carried = (
            passed_along(carried.astype(jnp.bfloat16), "ctx", -1).astype(carried.dtype)
            + partials[turn]
        )
    summed = passed_along(carried.astype(jnp.bfloat16), "ctx", reach_runs).astype(carried.dtype)
    first_sum = lax.psum(first_part, "ctx")
    head_rows = summed[:, :block] + jnp.where(run_index == 0, first_sum, jnp.zeros_like(first_sum))
    summed = jnp.concatenate([head_rows, summed[:, block:]], axis=1)
    key_grad = (summed[0] * scale).astype(jnp.bfloat16)
    value_grad = summed[1].astype(jnp.bfloat16)
    return (attended, query_grad, key_grad, value_grad, weight_grad)


def solution(mesh):
    placed = (
        P("ctx", "head"),
        P("ctx", "head"),
        P("ctx", "head"),
        P("ctx", "head"),
        P(),
        P("ctx", "head"),
    )
    return jax.shard_map(
        local,
        mesh=mesh,
        in_specs=placed,
        out_specs=(
            P("ctx", "head"),
            P("ctx", "head"),
            P("ctx", "head"),
            P("ctx", "head"),
            P("ctx", "head"),
        ),
        check_vma=False,
    )
```

profile of v0, /device:TPU:16, one launch (start us, length us, event | category | flops | bytes accessed | tf_op | source)
XLA Modules:
  0.0 1288.9 jit_solution(8840881994418569092)
XLA Ops:
  8.1 1.1 copy.109
  9.2 1.1 copy.110
  12.3 8.1 collective-permute-start
  20.5 11.3 collective-permute-done
  31.7 1.2 collective-permute-start.1
  32.9 18.8 %collective-permute-done.1 = bf16[2,256,512]{1,2,0:T(8,128)(2,1)S(1)} collective-permute-done((bf16[2,256,512]{1,2,0:T(8,128)(2,1)S(1)}, bf16[2,256,512]{1,2,0:T(8,128)(2,1)S(1)}, u32[]{:S(2)}, u32[]{:S(2)}) %collective-permute-start.1) | collective-permute-done | bytes 524320 | tf_op jit(solution)/shard_map/ppermute | solution.py:13
  51.8 2.5 collective-permute-start.2
  54.4 16.7 %collective-permute-done.2 = bf16[2,256,512]{1,2,0:T(8,128)(2,1)S(1)} collective-permute-done((bf16[2,256,512]{1,2,0:T(8,128)(2,1)S(1)}, bf16[2,256,512]{1,2,0:T(8,128)(2,1)S(1)}, u32[]{:S(2)}, u32[]{:S(2)}) %collective-permute-start.2) | collective-permute-done | bytes 524320 | tf_op jit(solution)/shard_map/ppermute | solution.py:13
  71.4 16.7 %collective-permute-done.3 = bf16[2,256,512]{1,2,0:T(8,128)(2,1)S(1)} collective-permute-done((bf16[2,256,512]{1,2,0:T(8,128)(2,1)S(1)}, bf16[2,256,512]{1,2,0:T(8,128)(2,1)S(1)}, u32[]{:S(2)}, u32[]{:S(2)}) %collective-permute-start.3) | collective-permute-done | bytes 524320 | tf_op jit(solution)/shard_map/ppermute | solution.py:13
  88.4 525.0 %all-reduce.3.cloned.1.call-done = bf16[2,128,512]{1,2,0:T(8,128)(2,1)} async-done(((bf16[2,128,512]{1,2,0:T(8,128)(2,1)}), bf16[2,128,512]{1,2,0:T(8,128)(2,1)}) %all-reduce.3.cloned.1.call-update) | async-done | bytes 262160 | tf_op jit(solution)/shard_map/psum | solution.py:18
  613.4 1.6 fusion.41
  615.0 1.1 fusion.43
  616.3 1.2 fusion.40
  617.6 0.9 copy.162
  618.4 1.5 reshape.65
  619.9 2.1 copy.111
  622.0 1.3 reshape_squeeze.12
  623.4 1.1 fusion.42
  625.5 1.2 copy-done.14
  626.7 1.0 fusion.44
  628.6 4.8 convolution_convert_fusion.1
  633.3 1.8 copy.122
  635.1 1.2 fusion.47
  636.4 2.9 multiply_reduce_fusion
  641.5 5.0 convolution_convert_fusion
  646.8 6.1 convolution_bitcast_fusion
  652.9 9.3 copy.160
  662.2 0.9 copy-done.13
  663.1 2.5 convolution_bitcast_fusion.1
  665.6 4.6 reshape.62
  670.2 3.1 copy.137
  673.3 3.9 multiply_convert_fusion
  678.8 6.5 copy.133
  685.3 4.1 stack_reshape.12
  689.4 3.3 copy.136
  692.6 1.3 fusion.32
  693.9 2.3 collective-permute-start.5
  696.2 9.8 collective-permute-done.5
  706.2 4.9 collective-permute-start.6
  711.1 6.9 collective-permute-done.6
  718.1 7.1 collective-permute-start.7
  725.1 9.1 collective-permute-done.7
  734.4 6.8 collective-permute-start.8
  741.2 9.7 collective-permute-done.8
  751.9 0.8 copy.141
  752.7 10.9 collective-permute-done.9
  763.7 514.7 %all-reduce.5.cloned.1.call-done = f32[2,128,512]{1,2,0:T(8,128)} async-done(((f32[2,128,512]{1,2,0:T(8,128)}), f32[2,128,512]{1,2,0:T(8,128)}) %all-reduce.5.cloned.1.call-update) | async-done | bytes 524304 | tf_op jit(solution)/shard_map/psum | solution.py:144
  1278.4 1.1 slice_add_fusion
  (102 shorter events, 12.0 us)
Async XLA Ops:
  8.0 46.2 %copy-start = (s32[128,3]{0,1:T(4,128)S(1)}, s32[128,3]{0,1:T(4,128)}, u32[]{:S(2)}) copy-start(s32[128,3]{0,1:T(4,128)} %param.10) | copy-start | bytes 4612
  8.0 80.2 %copy-start.20 = (bf16[256,512]{1,0:T(8,128)(2,1)S(1)}, bf16[256,512]{1,0:T(8,128)(2,1)}, u32[]{:S(2)}) copy-start(bf16[256,512]{1,0:T(8,128)(2,1)} %param.6) | copy-start | bytes 786436
  8.0 605.4 %all-reduce.3.cloned.1.call-start = ((), (), s32[]{:S(2)}) async-start(), calls=%async_computation.2 | async-start | bytes 524288 | tf_op jit(solution)/shard_map/psum | solution.py:18
  11.1 617.5 %all-gather.5.cloned.1.call-start = ((), (), s32[]{:S(2)}) async-start(), calls=%async_computation.5 | async-start | bytes 2621440 | tf_op jit(solution)/shard_map/all_gather | solution.py:89
  11.6 616.9 %all-gather.3.cloned.1.call-start = ((), (), s32[]{:S(2)}) async-start(), calls=%async_computation.3 | async-start | bytes 4259840 | tf_op jit(solution)/shard_map/all_gather | solution.py:82
  12.2 1266.2 %all-reduce.5.cloned.1.call-start = ((), (), s32[]{:S(2)}) async-start(), calls=%async_computation.6 | async-start | bytes 1048576 | tf_op jit(solution)/shard_map/psum | solution.py:144
  12.3 19.4 %collective-permute-start = (bf16[2,256,512]{1,2,0:T(8,128)(2,1)S(1)}, bf16[2,256,512]{1,2,0:T(8,128)(2,1)S(1)}, u32[]{:S(2)}, u32[]{:S(2)}) collective-permute-start(bf16[2,256,512]{1,2,0:T(8,128)(2,1)S(1)} %pad_maximum_fusion.1), channel_id=1, source_target_pairs={{0,248},{4,252},{8,0},{12,4},{16,8},{20,12},{24,16},{28,20},{32,24... | collective-permute-start | bytes 1572872 | tf_op jit(solution)/shard_map/ppermute | solution.py:13
  31.7 20.0 %collective-permute-start.1 = (bf16[2,256,512]{1,2,0:T(8,128)(2,1)S(1)}, bf16[2,256,512]{1,2,0:T(8,128)(2,1)S(1)}, u32[]{:S(2)}, u32[]{:S(2)}) collective-permute-start(bf16[2,256,512]{1,2,0:T(8,128)(2,1)S(1)} %collective-permute-done), channel_id=1, source_target_pairs={{0,4},{4,8},{8,12},{12,16},{16,20},{20,24},{24,28},{28,32},{32,36}... | collective-permute-start | bytes 1572872 | tf_op jit(solution)/shard_map/ppermute | solution.py:13
  51.8 19.4 %collective-permute-start.2 = (bf16[2,256,512]{1,2,0:T(8,128)(2,1)S(1)}, bf16[2,256,512]{1,2,0:T(8,128)(2,1)S(1)}, u32[]{:S(2)}, u32[]{:S(2)}) collective-permute-start(bf16[2,256,512]{1,2,0:T(8,128)(2,1)S(1)} %collective-permute-done.1), channel_id=1, source_target_pairs={{0,4},{4,8},{8,12},{12,16},{16,20},{20,24},{24,28},{28,32},{32,36}... | collective-permute-start | bytes 1572872 | tf_op jit(solution)/shard_map/ppermute | solution.py:13
  71.1 17.0 %collective-permute-start.3 = (bf16[2,256,512]{1,2,0:T(8,128)(2,1)S(1)}, bf16[2,256,512]{1,2,0:T(8,128)(2,1)S(1)}, u32[]{:S(2)}, u32[]{:S(2)}) collective-permute-start(bf16[2,256,512]{1,2,0:T(8,128)(2,1)S(1)} %collective-permute-done.2), channel_id=1, source_target_pairs={{0,4},{4,8},{8,12},{12,16},{16,20},{20,24},{24,28},{28,32},{32,36}... | collective-permute-start | bytes 1572872 | tf_op jit(solution)/shard_map/ppermute | solution.py:13
  88.2 527.9 %collective-permute-start.4 = (bf16[2,256,512]{1,2,0:T(8,128)(2,1)S(1)}, bf16[2,256,512]{1,2,0:T(8,128)(2,1)S(1)}, u32[]{:S(2)}, u32[]{:S(2)}) collective-permute-start(bf16[2,256,512]{1,2,0:T(8,128)(2,1)S(1)} %collective-permute-done.3), channel_id=1, source_target_pairs={{0,4},{4,8},{8,12},{12,16},{16,20},{20,24},{24,28},{28,32},{32,36}... | collective-permute-start | bytes 1572872 | tf_op jit(solution)/shard_map/ppermute | solution.py:13
  88.4 527.9 %copy-start.8 = (bf16[256,512]{0,1:T(8,128)(2,1)}, bf16[256,512]{0,1:T(8,128)(2,1)S(1)}, u32[]{:S(2)}) copy-start(bf16[256,512]{0,1:T(8,128)(2,1)S(1)} %copy.163) | copy-start | bytes 786436
  619.9 3.5 copy-start.4
  619.9 3.5 copy-start.9
  623.4 1.2 copy-start.11
  624.5 3.2 copy-start.3
  624.7 2.1 copy-start.18
  625.5 1.2 copy-start.14
  636.4 3.0 copy-start.12
  636.4 2.9 copy-start.19
  639.6 0.7 copy-start.16
  641.4 639.9 %reduce-scatter.5.cloned.1.call-start = ((), (), s32[]{:S(2)}) async-start(), calls=%async_computation.4 | async-start | bytes 2621440 | tf_op jit(solution)/shard_map/reduce_scatter | solution.py:86
  641.5 5.3 copy-start.15
  646.5 634.8 %reduce-scatter.7.cloned.1.call-start = ((), (), s32[]{:S(2)}) async-start(), calls=%async_computation.7 | async-start | bytes 8519680
  662.2 0.9 copy-start.13
  670.2 3.1 copy-start.10
  677.2 1.6 copy-start.6
  692.6 13.4 %copy-start.2 = (f32[5,1,256,512]{2,3,1,0:T(8,128)S(1)}, f32[5,1,256,512]{2,3,1,0:T(8,128)}, u32[]{:S(2)}) copy-start(f32[5,1,256,512]{2,3,1,0:T(8,128)} %copy.136) | copy-start | bytes 7864324
  693.9 12.1 collective-permute-start.5
  706.2 11.7 collective-permute-start.6
  718.1 16.2 %collective-permute-start.7 = (bf16[2,256,512]{1,2,0:T(8,128)(2,1)S(1)}, bf16[2,256,512]{1,2,0:T(8,128)(2,1)S(1)}, u32[]{:S(2)}, u32[]{:S(2)}) collective-permute-start(bf16[2,256,512]{1,2,0:T(8,128)(2,1)S(1)} %fusion.24), channel_id=1, source_target_pairs={{0,252},{4,0},{8,4},{12,8},{16,12},{20,16},{24,20},{28,24},{32,28}... | collective-permute-start | bytes 1572872 | tf_op jit(solution)/shard_map/ppermute | solution.py:13
  734.4 16.7 %copy-start.17 = (bf16[4,256,128]{1,2,0:T(8,128)(2,1)S(1)}, bf16[4,256,128]{1,2,0:T(8,128)(2,1)}, u32[]{:S(2)}) copy-start(bf16[4,256,128]{1,2,0:T(8,128)(2,1)} %copy-done.16) | copy-start | bytes 786436
  734.4 16.9 %copy-start.5 = (bf16[1280,4,128]{0,2,1:T(8,128)(2,1)S(1)}, bf16[1280,4,128]{0,2,1:T(8,128)(2,1)}, u32[]{:S(2)}) copy-start(bf16[1280,4,128]{0,2,1:T(8,128)(2,1)} %copy-done.4) | copy-start | bytes 3932164
  734.4 16.9 %copy-start.7 = (bf16[4,256,1280]{1,2,0:T(8,128)(2,1)S(1)}, bf16[4,256,1280]{1,2,0:T(8,128)(2,1)}, u32[]{:S(2)}) copy-start(bf16[4,256,1280]{1,2,0:T(8,128)(2,1)} %copy-done.6) | copy-start | bytes 7864324
  734.4 16.5 %collective-permute-start.8 = (bf16[2,256,512]{1,2,0:T(8,128)(2,1)S(1)}, bf16[2,256,512]{1,2,0:T(8,128)(2,1)S(1)}, u32[]{:S(2)}, u32[]{:S(2)}) collective-permute-start(bf16[2,256,512]{1,2,0:T(8,128)(2,1)S(1)} %fusion.14), channel_id=1, source_target_pairs={{0,252},{4,0},{8,4},{12,8},{16,12},{20,16},{24,20},{28,24},{32,28}... | collective-permute-start | bytes 1572872 | tf_op jit(solution)/shard_map/ppermute | solution.py:13
  751.0 12.6 collective-permute-start.9
  763.6 517.7 %copy-start.1 = (s32[128,3]{0,1:T(4,128)S(1)}, s32[128,3]{0,1:T(4,128)}, u32[]{:S(2)}) copy-start(s32[128,3]{0,1:T(4,128)} %param.10) | copy-start | bytes 4612
Sparse Core Ops, SparseCore 0:
  12.0 601.3 all-reduce.2
  641.6 636.8 all-reduce.4
Sparse Core Ops, SparseCore 1:
  13.4 37.5 all-gather.4
  52.6 333.4 all-gather.2
  646.6 43.9 reduce-scatter.4
  693.6 356.1 reduce-scatter.6
where the time goes:
time: 1290 us
  waiting for transfers between devices  1150 us (89%)
  local copies, waits for them, and re-layouts  50.4 us (4%)
  starting transfers between devices  33.4 us (3%)
  matrix products  31.6 us (2%)
  between operations  16.2 us (1%)
    psum x1, waiting for transfers between devices, spread(): return lax.psum(kept, axis)  525 us
    psum x1, waiting for transfers between devices, local(): first_sum = lax.psum(first_part, 'ctx')  515 us
    ppermute x10, waiting for transfers between devices, passed_along(): return lax.ppermute(x, axis, [(i, (i + by) % peers) for i in range(peers)])  110 us
    ppermute x10, starting transfers between devices, passed_along(): return lax.ppermute(x, axis, [(i, (i + by) % peers) for i in range(peers)])  33 us
  transfers between devices with their start and end apart: 16, of which 11 were waited for; matrix products, arithmetic and copies ran while one was open for 5% of the time, Pallas kernels for 0%

commit v1 on v0

v1 whole, which is shorter than its diff:
```python
import jax
import jax.numpy as jnp
from jax import lax
from jax.experimental import pallas as pl
from jax.experimental.pallas import tpu as pltpu
from jax.sharding import PartitionSpec as P

HD = 128
BLK = 128
SCALE = HD ** -0.5
BF = jnp.bfloat16
F32 = jnp.float32
NX, NZ, NY = 4, 8, 4
N_COPIES_A = 80
N_COPIES_B = 64


def place():
    i = lax.axis_index("ctx")
    h = lax.axis_index("head")
    cell = i // 2
    return cell // NZ, cell % NZ, (h // 2) * 2 + i % 2, h % 2, cell


def device(x, z, y, core):
    return ((x * NZ + z) * 2 + y % 2, (y // 2) * 2 + core)


def rows(start, size):
    return pl.ds(pl.multiple_of(start, size), size)


class Copies:
    def __init__(self, send, recv):
        self.send, self.recv, self.count = send, recv, 0

    def make(self, src, dst, target):
        k = self.count
        self.count += 1
        return pltpu.make_async_remote_copy(
            src_ref=src,
            dst_ref=dst,
            send_sem=self.send.at[k],
            recv_sem=self.recv.at[k],
            device_id=target,
            device_id_type=pl.DeviceIdType.MESH,
        )

    def start(self, src, dst, target):
        c = self.make(src, dst, target)
        c.start()
        return c


def greet(peers):
    barrier = pltpu.get_barrier_semaphore()
    for peer in peers:
        pl.semaphore_signal(
            barrier, inc=1, device_id=peer, device_id_type=pl.DeviceIdType.MESH
        )
    pl.semaphore_wait(barrier, len(peers))


def all_peers(x, z, y, core, cell):
    up, down = (cell + 1) % (NX * NZ), (cell + NX * NZ - 1) % (NX * NZ)
    peers = [device((x + d) % NX, z, y, core) for d in range(1, NX)]
    peers += [device(x, (z + d) % NZ, y, core) for d in range(1, NZ)]
    peers += [device(x, z, (y + d) % NY, core) for d in (1, NY - 1)]
    peers += [device(x, z, y, 1 - core)]
    peers += [device(c // NZ, c % NZ, y, core) for c in (up, down)]
    return peers


def gather_kernel(q, k, v, w, og, q2, kb, vb, b0, wf, ogf, send, recv, lsem):
    x, z, y, core, cell = place()
    ylo = y % 2
    h = (y // 2) * 2 + core
    x_up, x_dn = (x + 1) % NX, (x + NX - 1) % NX
    z_up, z_dn = (z + 1) % NZ, (z + NZ - 1) % NZ
    y_up, y_dn = (y + 1) % NY, (y + NY - 1) % NY
    c_up, c_dn = (cell + 1) % (NX * NZ), (cell + NX * NZ - 1) % (NX * NZ)
    mate = device(x, z, (y // 2) * 2 + 1 - ylo, core)
    twin = device(x, z, y, 1 - core)
    xu, xd = device(x_up, z, y, core), device(x_dn, z, y, core)
    zu, zd = device(x, z_up, y, core), device(x, z_dn, y, core)
    yu, yd = device(x, z, y_up, core), device(x, z, y_dn, core)
    cu, cd = device(c_up // NZ, c_up % NZ, y, core), device(c_dn // NZ, c_dn % NZ, y, core)
    net = Copies(send, recv)
    mine, other = rows(256 * ylo, 256), rows(256 * (1 - ylo), 256)

    locals_ = [
        pltpu.make_async_copy(w.at[:, mine], wf.at[x, z, rows(64 * ylo, 64), :], lsem.at[0]),
        pltpu.make_async_copy(k.at[:, mine], kb.at[1, mine, :], lsem.at[1]),
        pltpu.make_async_copy(v.at[:, mine], vb.at[1, mine, :], lsem.at[2]),
        pltpu.make_async_copy(q.at[:, mine], q2.at[mine, :], lsem.at[3]),
        pltpu.make_async_copy(og, ogf.at[ylo, h], lsem.at[4]),
    ]
    for c in locals_:
        c.start()
    greet(all_peers(x, z, y, core, cell))

    ends = []

    def go(src, dst, target):
        c = net.start(src, dst, target)
        ends.append(c)
        return c

    w_mate = go(w.at[:, other], wf.at[x, z, rows(64 * ylo, 64), :], mate)
    k_mate = go(k.at[:, other], kb.at[1, mine, :], mate)
    v_mate = go(v.at[:, other], vb.at[1, mine, :], mate)
    og_up = go(og, ogf.at[ylo, h], yu)
    og_dn = go(og, ogf.at[ylo, h], yd)
    og_tw = [go(og, ogf.at[ylo, h], twin)]
    q_mate = go(q.at[:, other], q2.at[mine, :], mate)

    locals_[0].wait()
    w_mate.wait_recv()

    x_plus, x_minus = {}, {}

    def to_x(off):
        zz = (z + off) % NZ
        x_plus[off] = go(wf.at[x, zz], wf.at[x, zz], xu)
        x_minus[off] = go(wf.at[x, zz], wf.at[x, zz], xd)

    up = go(wf.at[x, z], wf.at[x, z], zu)
    dn = go(wf.at[x, z], wf.at[x, z], zd)
    to_x(0)
    halo = [
        go(k.at[:, mine], kb.at[0, mine, :], cu),
        go(k.at[:, mine], kb.at[2, mine, :], cd),
    ]

    def ring_step(s, up, dn):
        zm, zp = (z + NZ - s) % NZ, (z + s) % NZ
        up.wait_recv()
        if s < 3:
            up = go(wf.at[x, zm], wf.at[x, zm], zu)
        else:
            up = go(wf.at[x, zm, 0:64, :], wf.at[x, zm, 0:64, :], zu)
        to_x(NZ - s)
        dn.wait_recv()
        if s < 3:
            dn = go(wf.at[x, zp], wf.at[x, zp], zd)
        else:
            dn = go(wf.at[x, zp, 64:128, :], wf.at[x, zp, 64:128, :], zd)
        to_x(s)
        return up, dn

    up, dn = ring_step(1, up, dn)
    halo += [
        go(v.at[:, mine], vb.at[0, mine, :], cu),
        go(v.at[:, mine], vb.at[2, mine, :], cd),
    ]
    k_mate.wait_recv()
    v_mate.wait_recv()
    locals_[1].wait()
    locals_[2].wait()

    along_z = []
    for d in range(1, NZ):
        target = device(x, (z + d) % NZ, y, core)
        along_z.append(
            (
                net.make(kb.at[1, 0:BLK, :], b0.at[0], target),
                net.make(vb.at[1, 0:BLK, :], b0.at[1], target),
            )
        )
    b_loc = [
        pltpu.make_async_copy(kb.at[1, 0:BLK, :], b0.at[0], lsem.at[5]),
        pltpu.make_async_copy(vb.at[1, 0:BLK, :], b0.at[1], lsem.at[6]),
    ]

    @pl.when(cell == 0)
    def _():
        for d in (4, 5, 3, 6, 2, 7, 1):
            for c in along_z[d - 1]:
                c.start()
        for c in b_loc:
            c.start()

    up, dn = ring_step(2, up, dn)
    halo += [
        go(kb.at[1, other, :], kb.at[0, other, :], cu),
        go(kb.at[1, other, :], kb.at[2, other, :], cd),
    ]
    up, dn = ring_step(3, up, dn)
    halo += [
        go(vb.at[1, other, :], vb.at[0, other, :], cu),
        go(vb.at[1, other, :], vb.at[2, other, :], cd),
    ]

    og_up.wait_recv()
    src_dn = ogf.at[y_dn % 2, (y_dn // 2) * 2 + core]
    fwd_up = go(src_dn.at[0:128, :], src_dn.at[0:128, :], yu)
    og_tw.append(go(src_dn, src_dn, twin))
    og_dn.wait_recv()
    src_up = ogf.at[y_up % 2, (y_up // 2) * 2 + core]
    fwd_dn = go(src_up.at[128:256, :], src_up.at[128:256, :], yd)
    og_tw.append(go(src_up, src_up, twin))

    up.wait_recv()
    dn.wait_recv()
    to_x(4)

    along_x = []
    for d in range(1, NX):
        along_x.append(net.make(b0, b0, device((x + d) % NX, z, y, core)))

    x_fwd = []
    for off in (0, 7, 1, 6, 2, 5, 3, 4):
        zz = (z + off) % NZ
        x_plus[off].wait_recv()
        if off in (0, 6, 2, 4):
            x_fwd.append(go(wf.at[x_dn, zz], wf.at[x_dn, zz], xu))
        x_minus[off].wait_recv()
        if off in (7, 1, 5, 3):
            x_fwd.append(go(wf.at[x_up, zz], wf.at[x_up, zz], xd))
        if off == 1:

            @pl.when((x == 0) & (z != 0))
            def _():
                for d in range(1, NZ):

                    @pl.when(z == d)
                    def _():
                        for c in along_z[d - 1]:
                            c.wait_recv()

            @pl.when(cell == 0)
            def _():
                for c in b_loc:
                    c.wait()

            @pl.when(x == 0)
            def _():
                for c in along_x:
                    c.start()

    fwd_up.wait_recv()
    fwd_dn.wait_recv()
    far = ogf.at[y % 2, ((y + 2) % NY // 2) * 2 + core]
    og_tw.append(go(far, far, twin))

    for c in halo + [q_mate] + x_fwd + og_tw:
        c.wait_recv()

    for d in range(1, NX):

        @pl.when(x == d)
        def _():
            along_x[d - 1].wait_recv()

    for c in ends:
        c.wait_send()

    @pl.when(cell == 0)
    def _():
        for pair in along_z:
            for c in pair:
                c.wait_send()

    @pl.when(x == 0)
    def _():
        for c in along_x:
            c.wait_send()

    locals_[3].wait()
    locals_[4].wait()


def compute_kernel(
    lists, q2, kb, vb, b0, wf, ogf, at, wg, dq, dke, dko, dve, dvo, d0, probs, mixed, mgrad, dk, dv
):
    cell = lax.axis_index("ctx") // 2
    nt = (((1,), (1,)), ((), ()))
    tn = (((0,), (0,)), ((), ()))

    def dot(a, b, dims=(((1,), (0,)), ((), ()))):
        return lax.dot_general(a, b, dims, preferred_element_type=F32)

    def picks(b):
        i = b - 4 * cell
        near = [(i + 4 + d, (b + d >= 1) & (b + d <= 127)) for d in (-1, 0, 1)]
        named = [lists[b, r] for r in range(3)]
        far = []
        for r, n in enumerate(named):
            good = (n >= 1) & ((n < b - 1) | (n > b + 1))
            for m in named[:r]:
                good = good & (n != m)
            far.append((n - 4 * cell + 4, good))
        return near + far

    def tiles(ref, first, found, lanes):
        return jnp.concatenate([first[:, lanes]] + [ref[j, :, lanes] for j, _ in found], axis=0)

    def forward(n, carry):
        i, head = n // 2, n % 2
        lanes = rows(128 * head, 128)
        toks = rows(128 * i, 128)
        found = picks(4 * cell + i)
        keys = tiles(kb, b0.at[0], found, lanes)
        values = tiles(vb, b0.at[1], found, lanes)
        bias = jnp.concatenate(
            [jnp.zeros((1, BLK), F32)]
            + [jnp.full((1, BLK), jnp.where(good, 0.0, -jnp.inf), F32) for _, good in found],
            axis=1,
        )
        s = dot(q2[toks, lanes], keys, nt) * SCALE + bias
        e = jnp.exp(s - jnp.max(s, axis=1, keepdims=True))
        p = e / jnp.sum(e, axis=1, keepdims=True)
        probs[n] = p
        mixed[toks, lanes] = dot(p.astype(BF), values).astype(BF)
        return carry

    lax.fori_loop(0, 8, forward, 0)

    for t in range(2):
        total = jnp.zeros((256, 256), F32)
        for h in range(4):
            total = total + dot(ogf[t, h], wf[h])
        mgrad[256 * t : 256 * (t + 1), :] = total.astype(BF)

    def project(h, carry):
        for t in range(2):
            at[t, h] = dot(mixed[256 * t : 256 * (t + 1), :], wf[h], nt).astype(BF)
        total = dot(mixed[0:256, :], ogf[0, h], tn) + dot(mixed[256:512, :], ogf[1, h], tn)
        for n in range(8):
            wg[h, n] = total[:, 128 * n : 128 * (n + 1)].astype(BF)
        return carry

    lax.fori_loop(0, 4, project, 0)

    dk[...] = jnp.zeros_like(dk)
    dv[...] = jnp.zeros_like(dv)

    def backward(n, carry):
        i, head = n // 2, n % 2
        lanes = rows(128 * head, 128)
        toks = rows(128 * i, 128)
        found = picks(4 * cell + i)
        keys = tiles(kb, b0.at[0], found, lanes)
        values = tiles(vb, b0.at[1], found, lanes)
        g = mgrad[toks, lanes]
        delta = jnp.sum(
            g.astype(F32) * mixed[toks, lanes].astype(F32), axis=1, keepdims=True
        )
        p = probs[n]
        slopes = (p * (dot(g, values, nt) - delta)).astype(BF)
        dq[toks, lanes] = (dot(slopes, keys) * SCALE).astype(BF)
        part_k = dot(slopes, q2[toks, lanes], tn)
        part_v = dot(p.astype(BF), g, tn)
        for m, j in enumerate([12] + [j for j, _ in found]):
            dk[j, :, lanes] += part_k[BLK * m : BLK * (m + 1)]
            dv[j, :, lanes] += part_v[BLK * m : BLK * (m + 1)]
        return carry

    lax.fori_loop(0, 8, backward, 0)
    for n in range(4):
        toks = slice(128 * n, 128 * (n + 1))
        dke[0, toks, :] = (dk[n] * SCALE).astype(BF)
        dko[toks, :] = dk[n + 4] * SCALE
        dke[1, toks, :] = (dk[n + 8] * SCALE).astype(BF)
        dve[0, toks, :] = dv[n].astype(BF)
        dvo[toks, :] = dv[n + 4]
        dve[1, toks, :] = dv[n + 8].astype(BF)
    d0[0] = (dk[12] * SCALE).astype(BF)
    d0[1] = dv[12].astype(BF)


def reduce_kernel(
    at, wg, dq, dke, dko, dve, dvo, d0,
    o_at, o_dq, o_dk, o_dv, o_wg,
    at_core, at_sum, at_r1, at_r2, wg_r1, wg_s, wg_r2, wg_x, wz_s, wz_r, w_out,
    dk_r, dv_r, d0_xr, d0_s, d0_zr, dkv_s, send, recv, lsem,
):
    x, z, y, core, cell = place()
    ylo = y % 2
    x_up, x_dn, x_far = (x + 1) % NX, (x + NX - 1) % NX, (x + 2) % NX
    z_up, z_dn = (z + 1) % NZ, (z + NZ - 1) % NZ
    y_up, y_dn, y_far = (y + 1) % NY, (y + NY - 1) % NY, (y + 2) % NY
    c_up, c_dn = (cell + 1) % (NX * NZ), (cell + NX * NZ - 1) % (NX * NZ)
    mate = device(x, z, (y // 2) * 2 + 1 - ylo, core)
    twin = device(x, z, y, 1 - core)
    xu, xd = device(x_up, z, y, core), device(x_dn, z, y, core)
    zu, zd = device(x, z_up, y, core), device(x, z_dn, y, core)
    yu, yd = device(x, z, y_up, core), device(x, z, y_dn, core)
    cu, cd = device(c_up // NZ, c_up % NZ, y, core), device(c_dn // NZ, c_dn % NZ, y, core)
    net = Copies(send, recv)
    mine, other = rows(256 * ylo, 256), rows(256 * (1 - ylo), 256)
    ends = []

    def go(src, dst, target):
        c = net.start(src, dst, target)
        ends.append(c)
        return c

    q_loc = pltpu.make_async_copy(dq.at[mine, :], o_dq.at[:, mine], lsem.at[0])
    q_loc.start()
    greet(all_peers(x, z, y, core, cell))

    w1u = go(wg.at[x_far, 0:4], wg_r1.at[0], xu)
    w1d = go(wg.at[x_far, 4:8], wg_r1.at[1], xd)
    order = (y_far, y_up, y_dn, y)
    cores = [
        go(at.at[t % 2, (t // 2) * 2 + 1 - core], at_core.at[t], twin) for t in order
    ]
    w2u = [go(wg.at[x_up, 4:8], wg_r2.at[0, 4:8], xu)]
    w2d = [go(wg.at[x_dn, 0:4], wg_r2.at[1, 0:4], xd)]
    to_x0 = [net.make(d0, d0_xr.at[d - 1], device(0, z, y, core)) for d in range(1, NX)]
    for d in range(1, NX):

        @pl.when(x == d)
        def _():
            to_x0[d - 1].start()

    edges = [
        go(dke.at[0], dk_r.at[1], cd),
        go(dke.at[1], dk_r.at[0], cu),
        go(dve.at[0], dv_r.at[1], cd),
        go(dve.at[1], dv_r.at[0], cu),
    ]
    q_mate = go(dq.at[other, :], o_dq.at[:, mine], mate)

    def add(n, dst, *srcs):
        def body(i, carry):
            r = rows(32 * i, 32)
            total = srcs[0][r, :].astype(F32)
            for s in srcs[1:]:
                total = total + s[r, :].astype(F32)
            dst[r, :] = total.astype(dst.dtype)
            return carry

        lax.fori_loop(0, n, body, 0)

    for n, t in enumerate(order):
        cores[n].wait_recv()
        add(8, at_sum.at[t], at.at[t % 2, (t // 2) * 2 + core], at_core.at[t])
        if n == 0:
            a1u = go(at_sum.at[t, 0:128, :], at_r1.at[0], yu)
            a1d = go(at_sum.at[t, 128:256, :], at_r1.at[1], yd)
        if n == 1:
            a2u = [go(at_sum.at[t, 128:256, :], at_r2.at[0, 128:256, :], yu)]
        if n == 2:
            a2d = [go(at_sum.at[t, 0:128, :], at_r2.at[1, 0:128, :], yd)]

    w1u.wait_recv()
    for n in range(4):
        add(8, wg_s.at[0, n], wg.at[x_up, n], wg_r1.at[0, n])
    w2u.append(go(wg_s.at[0], wg_r2.at[0, 0:4], xu))
    w1d.wait_recv()
    for n in range(4):
        add(8, wg_s.at[1, n], wg.at[x_dn, 4 + n], wg_r1.at[1, n])
    w2d.append(go(wg_s.at[1], wg_r2.at[1, 4:8], xd))

    a1u.wait_recv()
    add(4, at_s2_up := at_core.at[0, 0:128, :], at_sum.at[y_up, 0:128, :], at_r1.at[0])
    a2u.append(go(at_s2_up, at_r2.at[0, 0:128, :], yu))
    a1d.wait_recv()
    add(4, at_s2_dn := at_core.at[1, 128:256, :], at_sum.at[y_dn, 128:256, :], at_r1.at[1])
    a2d.append(go(at_s2_dn, at_r2.at[1, 128:256, :], yd))

    to_z0 = [net.make(d0_s, d0_zr.at[d - 1], device(x, 0, y, core)) for d in range(1, NZ)]

    @pl.when(x == 0)
    def _():
        for c in to_x0:
            c.wait_recv()
        for n in range(2):
            add(4, d0_s.at[n], d0.at[n], d0_xr.at[0, n], d0_xr.at[1, n], d0_xr.at[2, n])
        for d in range(1, NZ):

            @pl.when(z == d)
            def _():
                to_z0[d - 1].start()

    for c in w2u + w2d:
        c.wait_recv()
    for n in range(NZ):
        add(8, wg_x.at[n], wg.at[x, n], wg_r2.at[0, n], wg_r2.at[1, n])

    zf = (z + 4) % NZ
    add(4, wz_s.at[0, 0, 0:128, :], wg_x.at[zf, 0:128, :])
    up = go(wz_s.at[0, 0, 0:128, :], wz_r.at[0, 0, 0:128, :], zu)
    add(4, wz_s.at[1, 0, 128:256, :], wg_x.at[zf, 128:256, :])
    dn = go(wz_s.at[1, 0, 128:256, :], wz_r.at[1, 0, 128:256, :], zd)

    for c in edges:
        c.wait_recv()
    kv_mate = []

    @pl.when(cell == 0)
    def _():
        for c in to_z0:
            c.wait_recv()

    for n, (own, got) in enumerate(((dko, dk_r), (dvo, dv_r))):
        add(12, dkv_s.at[n, 128:512, :], own.at[128:512, :], got.at[0, 128:512, :], got.at[1, 128:512, :])

        @pl.when(cell == 0)
        def _():
            add(
                4, dkv_s.at[n, 0:128, :], own.at[0:128, :], got.at[0, 0:128, :],
                got.at[1, 0:128, :], d0_s.at[n], *[d0_zr.at[d, n] for d in range(NZ - 1)],
            )

        @pl.when(cell != 0)
        def _():
            add(4, dkv_s.at[n, 0:128, :], own.at[0:128, :], got.at[0, 0:128, :], got.at[1, 0:128, :])

    for s in (2, 3, 4):
        lo = 5 - s
        tu, td = (z + lo) % NZ, (z + NZ - lo) % NZ
        up.wait_recv()
        if s == 2:
            add(4, wz_s.at[0, 1, 0:128, :], wg_x.at[tu, 0:128, :], wz_r.at[0, 0, 0:128, :])
            add(4, wz_s.at[0, 1, 128:256, :], wg_x.at[tu, 128:256, :])
        else:
            add(8, wz_s.at[0, s - 1], wg_x.at[tu], wz_r.at[0, s - 2])
        up = go(wz_s.at[0, s - 1], wz_r.at[0, s - 1], zu)
        dn.wait_recv()
        if s == 2:
            add(4, wz_s.at[1, 1, 128:256, :], wg_x.at[td, 128:256, :], wz_r.at[1, 0, 128:256, :])
            add(4, wz_s.at[1, 1, 0:128, :], wg_x.at[td, 0:128, :])
        else:
            add(8, wz_s.at[1, s - 1], wg_x.at[td], wz_r.at[1, s - 2])
        dn = go(wz_s.at[1, s - 1], wz_r.at[1, s - 1], zd)
        if s == 2:
            for n, out in enumerate((o_dk, o_dv)):
                kv_mate.append(go(dkv_s.at[n, other, :], out.at[:, mine], mate))
                out[:, mine] = dkv_s[n, mine, :]
    up.wait_recv()
    dn.wait_recv()
    add(8, wg_x.at[z], wg_x.at[z], wz_r.at[0, 3], wz_r.at[1, 3])
    w_out[...] = wg_x[z].T
    w_mate = go(w_out.at[rows(64 * (1 - ylo), 64), :], o_wg.at[:, mine], mate)
    o_wg[:, mine] = w_out[rows(64 * ylo, 64), :]

    for c in a2u + a2d:
        c.wait_recv()
    add(8, o_at, at_sum.at[y], at_r2.at[0], at_r2.at[1])
    for c in kv_mate + [w_mate, q_mate]:
        c.wait_recv()
    q_loc.wait()

    for c in ends:
        c.wait_send()
    for d in range(1, NX):

        @pl.when(x == d)
        def _():
            to_x0[d - 1].wait_send()

    for d in range(1, NZ):

        @pl.when((x == 0) & (z == d))
        def _():
            to_z0[d - 1].wait_send()


def vmem(n):
    return [pl.BlockSpec(memory_space=pltpu.VMEM)] * n


def shape(dims, dtype=BF):
    return jax.ShapeDtypeStruct(dims, dtype)


def local(queries, key_heads, value_heads, out_weight, block_lists, out_grad):
    limit = 60 * 1024 * 1024
    q2, kb, vb, b0, wf, ogf = pl.pallas_call(
        gather_kernel,
        out_shape=(
            shape((512, 256)),
            shape((3, 512, 256)),
            shape((3, 512, 256)),
            shape((2, 128, 256)),
            shape((NX, NZ, 128, 256)),
            shape((2, 4, 256, 1024)),
        ),
        in_specs=vmem(5),
        out_specs=tuple(vmem(6)),
        scratch_shapes=[
            pltpu.SemaphoreType.DMA((N_COPIES_A,)),
            pltpu.SemaphoreType.DMA((N_COPIES_A,)),
            pltpu.SemaphoreType.DMA((8,)),
        ],
        compiler_params=pltpu.CompilerParams(
            collective_id=0, has_side_effects=True, vmem_limit_bytes=limit
        ),
        name="gather",
    )(queries, key_heads, value_heads, out_weight, out_grad)

    at, wg, dq, dke, dko, dve, dvo, d0 = pl.pallas_call(
        compute_kernel,
        out_shape=(
            shape((2, 4, 256, 1024)),
            shape((4, 8, 256, 128)),
            shape((512, 256)),
            shape((2, 512, 256)),
            shape((512, 256), F32),
            shape((2, 512, 256)),
            shape((512, 256), F32),
            shape((2, 128, 256)),
        ),
        in_specs=[pl.BlockSpec(memory_space=pltpu.SMEM)] + vmem(6),
        out_specs=tuple(vmem(8)),
        scratch_shapes=[
            pltpu.VMEM((8, 128, 896), F32),
            pltpu.VMEM((512, 256), BF),
            pltpu.VMEM((512, 256), BF),
            pltpu.VMEM((13, 128, 256), F32),
            pltpu.VMEM((13, 128, 256), F32),
        ],
        compiler_params=pltpu.CompilerParams(vmem_limit_bytes=limit),
        name="layer",
    )(
        block_lists,
        q2,
        kb.reshape(12, 128, 256),
        vb.reshape(12, 128, 256),
        b0,
        wf.reshape(4, 1024, 256),
        ogf,
    )

    return pl.pallas_call(
        reduce_kernel,
        out_shape=(
            shape((256, 1024)),
            shape((256, 512)),
            shape((256, 512)),
            shape((256, 512)),
            shape((64, 512), F32),
        ),
        in_specs=vmem(8),
        out_specs=tuple(vmem(5)),
        scratch_shapes=[
            pltpu.VMEM((4, 256, 1024), BF),
            pltpu.VMEM((4, 256, 1024), BF),
            pltpu.VMEM((2, 128, 1024), BF),
            pltpu.VMEM((2, 256, 1024), BF),
            pltpu.VMEM((2, 4, 256, 128), BF),
            pltpu.VMEM((2, 4, 256, 128), BF),
            pltpu.VMEM((2, 8, 256, 128), BF),
            pltpu.VMEM((8, 256, 128), F32),
            pltpu.VMEM((2, 4, 256, 128), BF),
            pltpu.VMEM((2, 4, 256, 128), BF),
            pltpu.VMEM((128, 256), F32),
            pltpu.VMEM((2, 512, 256), BF),
            pltpu.VMEM((2, 512, 256), BF),
            pltpu.VMEM((3, 2, 128, 256), BF),
            pltpu.VMEM((2, 128, 256), BF),
            pltpu.VMEM((7, 2, 128, 256), BF),
            pltpu.VMEM((2, 512, 256), BF),
            pltpu.SemaphoreType.DMA((N_COPIES_B,)),
            pltpu.SemaphoreType.DMA((N_COPIES_B,)),
            pltpu.SemaphoreType.DMA((2,)),
        ],
        compiler_params=pltpu.CompilerParams(
            collective_id=1, has_side_effects=True, vmem_limit_bytes=limit
        ),
        name="reduce",
    )(at, wg, dq, dke, dko, dve, dvo, d0)


def solution(mesh):
    placed = P("ctx", "head")
    return jax.shard_map(
        local,
        mesh=mesh,
        in_specs=(placed, placed, placed, placed, P(), placed),
        out_specs=(placed,) * 5,
        check_vma=False,
    )
```

time: 1290 us -> 145 us (0.11)
  waiting for transfers between devices: 1150 us -> 0 us
  Pallas kernels: 0 us -> 134 us
  local copies, waits for them, and re-layouts: 50.4 us -> 9.86 us
  starting transfers between devices: 33.4 us -> 0 us
  matrix products: 31.6 us -> 0 us
  between operations: 16.2 us -> 0.65 us
    psum x2 -> x0, waiting for transfers between devices: 1040 us -> none  [the longest x1 525 us: spread(): return lax.psum(kept, axis)]
    pallas_call x0 -> x3, Pallas kernels: none -> 134 us  [the longest x1 60.1 us: local(): pl.pallas_call(reduce_kernel, out_shape=(shape((256, 1024)), shape((256,...]
    ppermute x10 -> x0, waiting for transfers between devices: 110 us -> none  [passed_along(): return lax.ppermute(x, axis, [(i, (i + by) % peers) for i in range(peers)])]
    ppermute x10 -> x0, starting transfers between devices: 33 us -> none  [passed_along(): return lax.ppermute(x, axis, [(i, (i + by) % peers) for i in range(peers)])]
    dot_general x15 -> x0, matrix products: 31.6 us -> none  [the longest x1 6.09 us: local(): lax.dot_general(grad_full, mixed, (((0,), (0,)), ((), ())), preferred_ele...]
    another operation x8 -> x0, local copies, waits for them, and re-layouts: 18.7 us -> none  [the longest x4 15.1 us: local(): jnp.stack([band_dk.reshape(band_count, tok_dev, features), band_dv.reshap...]
  transfers between devices with their start and end apart: 16 -> 0, of which waited for: 11 -> 0; matrix products, arithmetic and copies ran while one was open for 5% -> 0% of each run, Pallas kernels for 0% -> 0%
where the time goes in v1:
time: 145 us
  Pallas kernels  134 us (92%)
  local copies, waits for them, and re-layouts  9.86 us (7%)
    pallas_call x1, Pallas kernels, local(): pl.pallas_call(reduce_kernel, out_shape=(shape((256, 1024)), shape((256,...  60.1 us
    pallas_call x1, Pallas kernels, local(): pl.pallas_call(gather_kernel, out_shape=(shape((512, 256)), shape((3, 512...  54.3 us
    pallas_call x1, Pallas kernels, local(): pl.pallas_call(compute_kernel, out_shape=(shape((2, 4, 256, 1024)), shape...  19.9 us
    unnamed x6, local copies, waits for them, and re-layouts  9.86 us

profile of v1, /device:TPU:16, one launch (start us, length us, event | category | flops | bytes accessed | tf_op | source)
XLA Modules:
  0.0 144.9 jit_solution(9340542641843294886)
XLA Ops:
  0.6 1.4 copy.11.lists
  2.0 54.3 %gather.1 = (bf16[512,256]{1,0:T(8,128)(2,1)}, bf16[3,512,256]{2,1,0:T(8,128)(2,1)}, bf16[3,512,256]{2,1,0:T(8,128)(2,1)}, bf16[2,128,256]{2,1,0:T(8,128)(2,1)},...) custom-call(bf16[256,512]{1,0:T(8,128)(2,1)} %q.1, bf16[256,512]{1,0:T(8,128)(2,1)} %k.1, ...), custom_call_target="tpu_custom_call" | custom-call | tf_op jit(solution)/shard_map/gather/pallas_call | solution.py:572
  56.3 19.9 %layer.1 = (bf16[2,4,256,1024]{3,2,1,0:T(8,128)(2,1)}, bf16[4,8,256,128]{3,2,1,0:T(8,128)(2,1)}, bf16[512,256]{1,0:T(8,128)(2,1)}, bf16[2,512,256]{2,1,0:T(8,128...) custom-call(s32[128,3]{1,0:T(8,128)} %copy.11.lists, ...), custom_call_target="tpu_custom_call" | custom-call | tf_op jit(solution)/shard_map/layer/pallas_call | solution.py:595
  76.3 60.1 %reduce.1 = (bf16[256,1024]{1,0:T(8,128)(2,1)}, bf16[256,512]{1,0:T(8,128)(2,1)}, bf16[256,512]{1,0:T(8,128)(2,1)}, bf16[256,512]{1,0:T(8,128)(2,1)}, f32[64,512]{1,0:T(8,128)}) custom-call(bf16[2,4,256,1024]{3,2,1,0:T(8,128)(2,1)} %get-tuple-element.25.at, bf16[4,8,256,128]{3,2,1,0:T(8,128)(2,1)} %get-tuple-element.26.wg, ...), custom_call_target="tpu_custom_call" | custom-call | tf_op jit(solution)/shard_map/reduce/pallas_call | solution.py:628
  136.4 1.9 %copy.17 = bf16[256,1024]{1,0:T(8,128)(2,1)} copy(bf16[256,1024]{1,0:T(8,128)(2,1)} %get-tuple-element.38) | data formatting | bytes 1048576
  138.3 1.7 %copy.18 = bf16[256,512]{1,0:T(8,128)(2,1)} copy(bf16[256,512]{1,0:T(8,128)(2,1)} %get-tuple-element.39) | data formatting | bytes 524288
  140.0 1.7 %copy.19 = bf16[256,512]{1,0:T(8,128)(2,1)} copy(bf16[256,512]{1,0:T(8,128)(2,1)} %get-tuple-element.40) | data formatting | bytes 524288
  141.6 1.7 %copy.20 = bf16[256,512]{1,0:T(8,128)(2,1)} copy(bf16[256,512]{1,0:T(8,128)(2,1)} %get-tuple-element.41) | data formatting | bytes 524288
  143.3 1.6 %copy.21 = f32[64,512]{1,0:T(8,128)} copy(f32[64,512]{1,0:T(8,128)} %get-tuple-element.42) | data formatting | bytes 262144

commit v2 on v0

v2 whole, which is shorter than its diff:
```python
import jax
import jax.numpy as jnp
from jax import lax
from jax.experimental import pallas as pl
from jax.experimental.pallas import tpu as pltpu
from jax.sharding import PartitionSpec as P

HD = 128
BLK = 128
SCALE = HD ** -0.5
BF = jnp.bfloat16
F32 = jnp.float32
NX, NZ, NY = 4, 8, 4
N_COPIES = 160


def place():
    i = lax.axis_index("ctx")
    h = lax.axis_index("head")
    cell = i // 2
    return cell // NZ, cell % NZ, (h // 2) * 2 + i % 2, h % 2, cell


def device(x, z, y, core):
    return ((x * NZ + z) * 2 + y % 2, (y // 2) * 2 + core)


def rows(start, size):
    return pl.ds(pl.multiple_of(start, size), size)


class Copies:
    def __init__(self, send, recv):
        self.send, self.recv, self.count = send, recv, 0

    def make(self, src, dst, target):
        k = self.count
        self.count += 1
        return pltpu.make_async_remote_copy(
            src_ref=src,
            dst_ref=dst,
            send_sem=self.send.at[k],
            recv_sem=self.recv.at[k],
            device_id=target,
            device_id_type=pl.DeviceIdType.MESH,
        )

    def start(self, src, dst, target):
        c = self.make(src, dst, target)
        c.start()
        return c


def greet(peers):
    barrier = pltpu.get_barrier_semaphore()
    for peer in peers:
        pl.semaphore_signal(
            barrier, inc=1, device_id=peer, device_id_type=pl.DeviceIdType.MESH
        )
    pl.semaphore_wait(barrier, len(peers))


def all_peers(x, z, y, core, cell):
    up, down = (cell + 1) % (NX * NZ), (cell + NX * NZ - 1) % (NX * NZ)
    peers = [device((x + d) % NX, z, y, core) for d in range(1, NX)]
    peers += [device(x, (z + d) % NZ, y, core) for d in range(1, NZ)]
    peers += [device(x, z, (y + d) % NY, core) for d in (1, NY - 1)]
    peers += [device(x, z, y, 1 - core)]
    peers += [device(c // NZ, c % NZ, y, core) for c in (up, down)]
    return peers


def dot(a, b, dims=(((1,), (0,)), ((), ()))):
    return lax.dot_general(a, b, dims, preferred_element_type=F32)


NT = (((1,), (1,)), ((), ()))
TN = (((0,), (0,)), ((), ()))


def add(dst, *srcs):
    n, lanes = dst.shape
    step = min(n, 16384 // lanes)

    def body(i, carry):
        r = rows(step * i, step)
        total = srcs[0][r, :].astype(F32)
        for s in srcs[1:]:
            total = total + s[r, :].astype(F32)
        dst[r, :] = total.astype(dst.dtype)
        return carry

    lax.fori_loop(0, n // step, body, 0)


def layer_kernel(
    q, k, v, w, lists_hbm, og,
    o_at, o_dq, o_dk, o_dv, o_wg,
    lists, q2, kb, vb, b0, wf, ogf, at, wg, probs, mixed, mgrad, dk, dv, d0, dq,
    at_core, at_sum, at_r1, at_r2, at_o, wg_r1, wg_s, wg_r2, wg_x, wz_s, wz_r, w_out,
    dke, dk_r, d0_b, d0_xr, d0_s, d0_zr, d0_t, d0_z0, dkv_s, d_out, send, recv, lsem,
):
    x, z, y, core, cell = place()
    ylo = y % 2
    h = (y // 2) * 2 + core
    x_up, x_dn, x_far = (x + 1) % NX, (x + NX - 1) % NX, (x + 2) % NX
    z_up, z_dn = (z + 1) % NZ, (z + NZ - 1) % NZ
    c_up, c_dn = (cell + 1) % (NX * NZ), (cell + NX * NZ - 1) % (NX * NZ)
    y_mate = y + 1 - 2 * ylo
    y_next = (y + NY - 1 + 2 * ylo) % NY
    y_far = (y + 2) % NY
    mate, nxt = device(x, z, y_mate, core), device(x, z, y_next, core)
    twin = device(x, z, y, 1 - core)
    xu, xd = device(x_up, z, y, core), device(x_dn, z, y, core)
    zu, zd = device(x, z_up, y, core), device(x, z_dn, y, core)
    cu, cd = device(c_up // NZ, c_up % NZ, y, core), device(c_dn // NZ, c_dn % NZ, y, core)
    net = Copies(send, recv)
    mine, other = rows(256 * ylo, 256), rows(256 * (1 - ylo), 256)
    band_mine, band_other = rows(512 + 256 * ylo, 256), rows(512 + 256 * (1 - ylo), 256)
    lo_mine, lo_other = mine, other
    hi_mine, hi_other = rows(1024 + 256 * ylo, 256), rows(1024 + 256 * (1 - ylo), 256)
    ends, n_local = [], [0]

    def go(src, dst, target):
        c = net.start(src, dst, target)
        ends.append(c)
        return c

    def here(src, dst):
        c = pltpu.make_async_copy(src, dst, lsem.at[n_local[0]])
        n_local[0] += 1
        return c

    def here_now(src, dst):
        c = here(src, dst)
        c.start()
        return c

    w_loc = here_now(w.at[:, mine], wf.at[x, z, rows(64 * ylo, 64), :])
    k_loc = here_now(k.at[:, mine], kb.at[band_mine, :])
    v_loc = here_now(v.at[:, mine], vb.at[band_mine, :])
    og_loc = here_now(og, ogf.at[ylo, h])
    q_loc = here_now(q.at[:, mine], q2.at[mine, :])
    list_loc = here_now(lists_hbm, lists)
    greet(all_peers(x, z, y, core, cell))

    w_mate = go(w.at[:, other], wf.at[x, z, rows(64 * ylo, 64), :], mate)
    k_mate = go(k.at[:, other], kb.at[band_mine, :], mate)
    v_mate = go(v.at[:, other], vb.at[band_mine, :], mate)
    og_next = go(og, ogf.at[ylo, h], nxt)
    og_mate = go(og, ogf.at[ylo, h], mate)
    og_tw = [go(og, ogf.at[ylo, h], twin)]
    q_mate = go(q.at[:, other], q2.at[mine, :], mate)

    w_loc.wait()
    w_mate.wait_recv()

    x_plus, x_minus = {}, {}

    def to_x(off):
        zz = (z + off) % NZ
        x_plus[off] = go(wf.at[x, zz], wf.at[x, zz], xu)
        x_minus[off] = go(wf.at[x, zz], wf.at[x, zz], xd)

    up = go(wf.at[x, z], wf.at[x, z], zu)
    dn = go(wf.at[x, z], wf.at[x, z], zd)
    to_x(0)
    halo = [
        go(k.at[:, mine], kb.at[lo_mine, :], cu),
        go(k.at[:, mine], kb.at[hi_mine, :], cd),
    ]

    def ring_step(s, up, dn):
        zm, zp = (z + NZ - s) % NZ, (z + s) % NZ
        up.wait_recv()
        if s < 3:
            up = go(wf.at[x, zm], wf.at[x, zm], zu)
        else:
            up = go(wf.at[x, zm, 0:64, :], wf.at[x, zm, 0:64, :], zu)
        to_x(NZ - s)
        dn.wait_recv()
        if s < 3:
            dn = go(wf.at[x, zp], wf.at[x, zp], zd)
        else:
            dn = go(wf.at[x, zp, 64:128, :], wf.at[x, zp, 64:128, :], zd)
        to_x(s)
        return up, dn

    up, dn = ring_step(1, up, dn)
    halo += [
        go(v.at[:, mine], vb.at[lo_mine, :], cu),
        go(v.at[:, mine], vb.at[hi_mine, :], cd),
    ]
    k_mate.wait_recv()
    v_mate.wait_recv()
    k_loc.wait()
    v_loc.wait()

    own_k0, own_v0 = kb.at[512 : 512 + BLK, :], vb.at[512 : 512 + BLK, :]
    tree = [
        (
            net.make(own_k0, b0.at[0], device(x, (z + d) % NZ, y, core)),
            net.make(own_v0, b0.at[1], device(x, (z + d) % NZ, y, core)),
        )
        for d in (1, 3, 5, 7)
    ]
    z_leaf = jnp.where(z == 7, 6, (z + 1) % NZ)
    leaf = net.make(b0, b0, device(x, z_leaf, y, core))
    b_loc = [here(own_k0, b0.at[0]), here(own_v0, b0.at[1])]
    along_x = [net.make(b0, b0, device((x + d) % NX, z, y, core)) for d in range(1, NX)]

    @pl.when(cell == 0)
    def _():
        for n in (1, 2, 0, 3):
            for c in tree[n]:
                c.start()
        for c in b_loc:
            c.start()

    up, dn = ring_step(2, up, dn)
    halo += [
        go(kb.at[band_other, :], kb.at[lo_other, :], cu),
        go(kb.at[band_other, :], kb.at[hi_other, :], cd),
    ]
    up, dn = ring_step(3, up, dn)
    halo += [
        go(vb.at[band_other, :], vb.at[lo_other, :], cu),
        go(vb.at[band_other, :], vb.at[hi_other, :], cd),
    ]

    cut = 224
    og_mate.wait_recv()
    from_mate = ogf.at[y_mate % 2, (y_mate // 2) * 2 + core]
    fwd_next = go(from_mate.at[0:cut, :], from_mate.at[0:cut, :], nxt)
    og_tw.append(go(from_mate, from_mate, twin))

    @pl.when(x == 0)
    def _():
        for n, d in enumerate((1, 3, 5, 7)):

            @pl.when(z == d)
            def _():
                for c in tree[n]:
                    c.wait_recv()

        @pl.when((z == 1) | (z == 3) | (z == 7))
        def _():
            leaf.start()

    up.wait_recv()
    dn.wait_recv()
    to_x(4)
    og_next.wait_recv()
    from_next = ogf.at[y_next % 2, (y_next // 2) * 2 + core]
    fwd_mate = go(from_next.at[cut:256, :], from_next.at[cut:256, :], mate)
    og_tw.append(go(from_next, from_next, twin))

    x_fwd = []

    def pass_x(off):
        zz = (z + off) % NZ
        x_plus[off].wait_recv()
        if off in (0, 6, 2, 4):
            x_fwd.append(go(wf.at[x_dn, zz], wf.at[x_dn, zz], xu))
        x_minus[off].wait_recv()
        if off in (7, 1, 5, 3):
            x_fwd.append(go(wf.at[x_up, zz], wf.at[x_up, zz], xd))

    for off in (0, 7, 1):
        pass_x(off)

    @pl.when((x == 0) & ((z == 2) | (z == 4) | (z == 6)))
    def _():
        leaf.wait_recv()

    @pl.when(cell == 0)
    def _():
        for c in b_loc:
            c.wait()

    @pl.when(x == 0)
    def _():
        for c in along_x:
            c.start()

    for off in (6, 2):
        pass_x(off)
    for c in halo + [q_mate]:
        c.wait_recv()
    q_loc.wait()
    list_loc.wait()
    for d in range(1, NX):

        @pl.when(x == d)
        def _():
            along_x[d - 1].wait_recv()

    def window(n):
        i, head = n % 4, n // 4
        return i, head, rows(128 * i, 128), pl.ds(pl.multiple_of(128 * i, 128), 1152), rows(128 * head, 128)

    def forward(n, carry):
        i, head, toks, win, lanes = window(n)
        b = 4 * cell + i
        bias = []
        for j in range(9):
            kbl = b - 4 + j
            good = (kbl >= 1) & (kbl <= 127)
            if j not in (3, 4, 5):
                named = (lists[b, 0] == kbl) | (lists[b, 1] == kbl) | (lists[b, 2] == kbl)
                good = good & named
            bias.append(jnp.full((1, BLK), jnp.where(good, 0.0, -jnp.inf), F32))
        bias = jnp.concatenate(bias, axis=1)
        qq = q2[toks, lanes]
        s0 = dot(qq, b0[0, :, lanes], NT) * SCALE
        s1 = dot(qq, kb[win, lanes], NT) * SCALE + bias
        top = jnp.maximum(jnp.max(s0, axis=1, keepdims=True), jnp.max(s1, axis=1, keepdims=True))
        e0, e1 = jnp.exp(s0 - top), jnp.exp(s1 - top)
        inv = 1.0 / (jnp.sum(e0, axis=1, keepdims=True) + jnp.sum(e1, axis=1, keepdims=True))
        p0, p1 = e0 * inv, e1 * inv
        probs[n, :, 0:BLK] = p0
        probs[n, :, BLK:] = p1
        out = dot(p0.astype(BF), b0[1, :, lanes]) + dot(p1.astype(BF), vb[win, lanes])
        mixed[toks, lanes] = out.astype(BF)
        return carry

    lax.fori_loop(0, 4, forward, 0)
    for off in (5, 3, 4):
        pass_x(off)
    fwd_next.wait_recv()
    fwd_mate.wait_recv()
    far = ogf.at[y_far % 2, (y_far // 2) * 2 + core]
    og_tw.append(go(far, far, twin))
    lax.fori_loop(4, 8, forward, 0)
    og_loc.wait()
    for c in og_tw:
        c.wait_recv()

    def weight_part(xx):
        total = dot(mixed[0:256, :], ogf[0, xx], TN) + dot(mixed[256:512, :], ogf[1, xx], TN)
        for n in range(8):
            wg[xx, n] = total[:, 128 * n : 128 * (n + 1)].astype(BF)

    def attended_part(t, c):
        hh = (t // 2) * 2 + c
        part = dot(mixed[rows(256 * (t % 2), 256), :], wf[hh].reshape(1024, 256), NT)
        at[t % 2, hh] = part.astype(BF)

    weight_part(x_far)
    w1u = go(wg.at[x_far, 0:4], wg_r1.at[0], xu)
    w1d = go(wg.at[x_far, 4:8], wg_r1.at[1], xd)
    weight_part(x_up)
    w2u = [go(wg.at[x_up, 4:8], wg_r2.at[0, 4:8], xu)]
    weight_part(x_dn)
    w2d = [go(wg.at[x_dn, 0:4], wg_r2.at[1, 0:4], xd)]
    for c in x_fwd:
        c.wait_recv()
    order = (y_far, y_mate, y_next, y)
    cores = []
    for t in order:
        attended_part(t, 1 - core)
        cores.append(go(at.at[t % 2, (t // 2) * 2 + 1 - core], at_core.at[t], twin))
    for t in order:
        attended_part(t, core)

    w1u.wait_recv()
    for n in range(4):
        add(wg_s.at[0, n], wg.at[x_up, n], wg_r1.at[0, n])
    w2u.append(go(wg_s.at[0], wg_r2.at[0, 0:4], xu))
    w1d.wait_recv()
    for n in range(4):
        add(wg_s.at[1, n], wg.at[x_dn, 4 + n], wg_r1.at[1, n])
    w2d.append(go(wg_s.at[1], wg_r2.at[1, 4:8], xd))

    for n, t in enumerate(order):
        cores[n].wait_recv()
        add(at_sum.at[t], at.at[t % 2, (t // 2) * 2 + core], at_core.at[t])
        if n == 0:
            a1n = go(at_sum.at[t, 0:128, :], at_r1.at[0], nxt)
            a1m = go(at_sum.at[t, 128:256, :], at_r1.at[1], mate)
        if n == 1:
            a2m = [go(at_sum.at[t, 128:256, :], at_r2.at[0, 128:256, :], mate)]
        if n == 2:
            a2n = [go(at_sum.at[t, 0:128, :], at_r2.at[1, 0:128, :], nxt)]
    weight_part(x)

    for t in range(2):
        total = jnp.zeros((256, 256), F32)
        for hh in range(4):
            total = total + dot(ogf[t, hh], wf[hh].reshape(1024, 256))
        mgrad[256 * t : 256 * (t + 1), :] = total.astype(BF)
    dk[...] = jnp.zeros_like(dk)
    dv[...] = jnp.zeros_like(dv)
    d0[...] = jnp.zeros_like(d0)

    def backward(n, carry):
        i, head, toks, win, lanes = window(n)
        g = mgrad[toks, lanes]
        delta = jnp.sum(
            g.astype(F32) * mixed[toks, lanes].astype(F32), axis=1, keepdims=True
        )
        p0, p1 = probs[n, :, 0:BLK], probs[n, :, BLK:]
        sl0 = (p0 * (dot(g, b0[1, :, lanes], NT) - delta)).astype(BF)
        sl1 = (p1 * (dot(g, vb[win, lanes], NT) - delta)).astype(BF)
        out = dot(sl0, b0[0, :, lanes]) + dot(sl1, kb[win, lanes])
        dq[toks, lanes] = (out * SCALE).astype(BF)
        qq = q2[toks, lanes]
        dk[win, lanes] += dot(sl1, qq, TN)
        dv[win, lanes] += dot(p1.astype(BF), g, TN)
        d0[0, :, lanes] += dot(sl0, qq, TN)
        d0[1, :, lanes] += dot(p0.astype(BF), g, TN)
        return carry

    edges, to_x0, q_out = [], [], []

    def leave(head):
        lanes = slice(128 * head, 128 * (head + 1))
        for n, (acc, factor) in enumerate(((dk, SCALE), (dv, 1.0))):
            dke[head, n, 0] = (acc[0:512, lanes] * factor).astype(BF)
            dke[head, n, 1] = (acc[1024:1536, lanes] * factor).astype(BF)
            d0_b[head, n] = (d0[n, :, lanes] * factor).astype(BF)
        edges.append(
            [go(dke.at[head, n, 0], dk_r.at[head, n, 1], cd) for n in range(2)]
            + [go(dke.at[head, n, 1], dk_r.at[head, n, 0], cu) for n in range(2)]
        )
        to_x0.append(
            [
                net.make(d0_b.at[head], d0_xr.at[head, d - 1], device(0, z, y, core))
                for d in range(1, NX)
            ]
        )
        for d in range(1, NX):

            @pl.when(x == d)
            def _():
                to_x0[head][d - 1].start()

        cols = rows(256 * ylo + 128 * head, 128)
        q_out.append(go(dq.at[other, lanes], o_dq.at[:, cols], mate))
        locals_out.append(here_now(dq.at[mine, lanes], o_dq.at[:, cols]))

    locals_out = []
    lax.fori_loop(0, 2, backward, 0)

    a1n.wait_recv()
    to_mate = at_core.at[0, 0:128, :]
    add(to_mate, at_sum.at[y_mate, 0:128, :], at_r1.at[0])
    a2m.append(go(to_mate, at_r2.at[0, 0:128, :], mate))
    a1m.wait_recv()
    to_next = at_core.at[1, 128:256, :]
    add(to_next, at_sum.at[y_next, 128:256, :], at_r1.at[1])
    a2n.append(go(to_next, at_r2.at[1, 128:256, :], nxt))

    lax.fori_loop(2, 4, backward, 0)
    leave(0)
    lax.fori_loop(4, 8, backward, 0)
    leave(1)

    for c in w2u + w2d:
        c.wait_recv()
    for n in range(NZ):
        add(wg_x.at[n], wg.at[x, n], wg_r2.at[0, n], wg_r2.at[1, n])

    zf = (z + 4) % NZ
    add(wz_s.at[0, 0, 0:128, :], wg_x.at[zf, 0:128, :])
    up = go(wz_s.at[0, 0, 0:128, :], wz_r.at[0, 0, 0:128, :], zu)
    add(wz_s.at[1, 0, 128:256, :], wg_x.at[zf, 128:256, :])
    dn = go(wz_s.at[1, 0, 128:256, :], wz_r.at[1, 0, 128:256, :], zd)

    z_stem = jnp.where(z == 6, 7, (z + NZ - 1) % NZ)
    stem = [net.make(d0_s.at[a], d0_zr.at[a], device(x, z_stem, y, core)) for a in range(2)]
    root = [
        [net.make(d0_t.at[a], d0_z0.at[a, n], device(x, 0, y, core)) for n in range(4)]
        for a in range(2)
    ]

    def sum_x(a):
        @pl.when(x == 0)
        def _():
            for c in to_x0[a]:
                c.wait_recv()
            for n in range(2):
                add(d0_s.at[a, n], d0_b.at[a, n], *[d0_xr.at[a, d, n] for d in range(3)])

            @pl.when((z == 2) | (z == 4) | (z == 6))
            def _():
                stem[a].start()

    def sum_z(a):
        @pl.when(x == 0)
        def _():
            @pl.when((z == 1) | (z == 3) | (z == 7))
            def _():
                stem[a].wait_recv()
                for n in range(2):
                    add(d0_t.at[a, n], d0_s.at[a, n], d0_zr.at[a, n])

            @pl.when(z == 5)
            def _():
                for n in range(2):
                    add(d0_t.at[a, n], d0_s.at[a, n])

            for n in range(4):

                @pl.when(z == 2 * n + 1)
                def _():
                    root[a][n].start()

    def z_step(s, up, dn):
        lo = 5 - s
        tu, td = (z + lo) % NZ, (z + NZ - lo) % NZ
        up.wait_recv()
        if s == 2:
            add(wz_s.at[0, 1, 0:128, :], wg_x.at[tu, 0:128, :], wz_r.at[0, 0, 0:128, :])
            add(wz_s.at[0, 1, 128:256, :], wg_x.at[tu, 128:256, :])
        else:
            add(wz_s.at[0, s - 1], wg_x.at[tu], wz_r.at[0, s - 2])
        up = go(wz_s.at[0, s - 1], wz_r.at[0, s - 1], zu)
        dn.wait_recv()
        if s == 2:
            add(wz_s.at[1, 1, 128:256, :], wg_x.at[td, 128:256, :], wz_r.at[1, 0, 128:256, :])
            add(wz_s.at[1, 1, 0:128, :], wg_x.at[td, 0:128, :])
        else:
            add(wz_s.at[1, s - 1], wg_x.at[td], wz_r.at[1, s - 2])
        dn = go(wz_s.at[1, s - 1], wz_r.at[1, s - 1], zd)
        return up, dn

    kv_mate, kv_here = [[], []], [[], []]

    def finish(head):
        for c in edges[head]:
            c.wait_recv()
        lanes = slice(128 * head, 128 * (head + 1))
        cols = rows(256 * ylo + 128 * head, 128)
        for n, (acc, factor) in enumerate(((dk, SCALE), (dv, 1.0))):
            dkv_s[n, :, lanes] = (
                acc[512:1024, lanes] * factor
                + dk_r[head, n, 0].astype(F32)
                + dk_r[head, n, 1].astype(F32)
            )
            out = (o_dk, o_dv)[n]
            kv_mate[head].append(net.make(d_out.at[n, other, lanes], out.at[:, cols], mate))
            kv_here[head].append(here(d_out.at[n, mine, lanes], out.at[:, cols]))

        @pl.when(cell != 0)
        def _():
            d_out[:, :, lanes] = dkv_s[:, :, lanes].astype(BF)
            for c in kv_mate[head] + kv_here[head]:
                c.start()

    sum_x(0)
    up, dn = z_step(2, up, dn)
    sum_x(1)
    finish(0)
    up, dn = z_step(3, up, dn)
    sum_z(0)
    sum_z(1)
    finish(1)
    up, dn = z_step(4, up, dn)

    @pl.when(cell == 0)
    def _():
        for head in range(2):
            lanes = slice(128 * head, 128 * (head + 1))
            for c in root[head]:
                c.wait_recv()
            for n in range(2):
                total = dkv_s[n, 0:BLK, lanes] + d0_s[head, n].astype(F32)
                for m in range(4):
                    total = total + d0_z0[head, m, n].astype(F32)
                dkv_s[n, 0:BLK, lanes] = total
            d_out[:, :, lanes] = dkv_s[:, :, lanes].astype(BF)
            for c in kv_mate[head] + kv_here[head]:
                c.start()

    for c in a2m + a2n:
        c.wait_recv()
    add(at_o, at_sum.at[y], at_r2.at[0], at_r2.at[1])
    locals_out.append(here_now(at_o, o_at))

    up.wait_recv()
    dn.wait_recv()
    add(wg_x.at[z], wg_x.at[z], wz_r.at[0, 3], wz_r.at[1, 3])
    w_out[...] = wg_x[z].T
    w_last = go(w_out.at[rows(64 * (1 - ylo), 64), :], o_wg.at[:, mine], mate)
    locals_out.append(here_now(w_out.at[rows(64 * ylo, 64), :], o_wg.at[:, mine]))

    for c in kv_mate[0] + kv_mate[1] + q_out + [w_last]:
        c.wait_recv()
    for c in locals_out + kv_here[0] + kv_here[1]:
        c.wait()
    for c in ends + kv_mate[0] + kv_mate[1]:
        c.wait_send()

    @pl.when(cell == 0)
    def _():
        for pair in tree:
            for c in pair:
                c.wait_send()

    @pl.when(x == 0)
    def _():
        for c in along_x:
            c.wait_send()

        @pl.when((z == 1) | (z == 3) | (z == 7))
        def _():
            leaf.wait_send()

        @pl.when((z == 2) | (z == 4) | (z == 6))
        def _():
            for c in stem:
                c.wait_send()

        for n in range(4):

            @pl.when(z == 2 * n + 1)
            def _():
                for a in range(2):
                    root[a][n].wait_send()

    for d in range(1, NX):

        @pl.when(x == d)
        def _():
            for a in range(2):
                to_x0[a][d - 1].wait_send()


def hand_over_kernel(*refs):
    n = 5
    ins, outs, bufs, sem = refs[:n], refs[n : 2 * n], refs[2 * n : 3 * n], refs[3 * n]
    reads = [pltpu.make_async_copy(ins[i], bufs[i], sem.at[0, i]) for i in range(n)]
    writes = [pltpu.make_async_copy(bufs[i], outs[i], sem.at[1, i]) for i in range(n)]
    for c in reads:
        c.start()
    for i in range(n):
        reads[i].wait()
        writes[i].start()
    for c in writes:
        c.wait()


def anywhere(n):
    return [pl.BlockSpec(memory_space=pl.ANY)] * n


def local(queries, key_heads, value_heads, out_weight, block_lists, out_grad):
    results = (
        jax.ShapeDtypeStruct((256, 1024), BF),
        jax.ShapeDtypeStruct((256, 512), BF),
        jax.ShapeDtypeStruct((256, 512), BF),
        jax.ShapeDtypeStruct((256, 512), BF),
        jax.ShapeDtypeStruct((64, 512), F32),
    )
    b, f = (lambda *s: pltpu.VMEM(s, BF)), (lambda *s: pltpu.VMEM(s, F32))
    scratch = [
        pltpu.SMEM((128, 3), jnp.int32),
        b(512, 256),
        b(1536, 256),
        b(1536, 256),
        b(2, 128, 256),
        b(NX, NZ, 128, 256),
        b(2, 4, 256, 1024),
        b(2, 4, 256, 1024),
        b(4, 8, 256, 128),
        f(8, 128, 1280),
        b(512, 256),
        b(512, 256),
        f(1536, 256),
        f(1536, 256),
        f(2, 128, 256),
        b(512, 256),
        b(4, 256, 1024),
        b(4, 256, 1024),
        b(2, 128, 1024),
        b(2, 256, 1024),
        b(256, 1024),
        b(2, 4, 256, 128),
        b(2, 4, 256, 128),
        b(2, 8, 256, 128),
        f(8, 256, 128),
        b(2, 4, 256, 128),
        b(2, 4, 256, 128),
        f(128, 256),
        b(2, 2, 2, 512, 128),
        b(2, 2, 2, 512, 128),
        b(2, 2, 128, 128),
        b(2, 3, 2, 128, 128),
        b(2, 2, 128, 128),
        b(2, 2, 128, 128),
        b(2, 2, 128, 128),
        b(2, 4, 2, 128, 128),
        f(2, 512, 256),
        b(2, 512, 256),
        pltpu.SemaphoreType.DMA((N_COPIES,)),
        pltpu.SemaphoreType.DMA((N_COPIES,)),
        pltpu.SemaphoreType.DMA((24,)),
    ]
    outs = pl.pallas_call(
        layer_kernel,
        out_shape=results,
        in_specs=anywhere(6),
        out_specs=tuple(anywhere(5)),
        scratch_shapes=scratch,
        compiler_params=pltpu.CompilerParams(
            collective_id=0, has_side_effects=True, vmem_limit_bytes=60 * 1024 * 1024
        ),
        name="layer",
    )(queries, key_heads, value_heads, out_weight, block_lists, out_grad)
    return pl.pallas_call(
        hand_over_kernel,
        out_shape=results,
        in_specs=anywhere(5),
        out_specs=tuple(anywhere(5)),
        scratch_shapes=[pltpu.VMEM(r.shape, r.dtype) for r in results]
        + [pltpu.SemaphoreType.DMA((2, 5))],
        name="hand_over",
    )(*outs)


def solution(mesh):
    placed = P("ctx", "head")
    return jax.shard_map(
        local,
        mesh=mesh,
        in_specs=(placed, placed, placed, placed, P(), placed),
        out_specs=(placed,) * 5,
        check_vma=False,
    )
```

time: 1290 us -> 104 us (0.08)
  waiting for transfers between devices: 1150 us -> 0 us
  Pallas kernels: 0 us -> 102 us
  local copies, waits for them, and re-layouts: 50.4 us -> 1.42 us
  starting transfers between devices: 33.4 us -> 0 us
  matrix products: 31.6 us -> 0 us
  between operations: 16.2 us -> 0.64 us
    psum x2 -> x0, waiting for transfers between devices: 1040 us -> none  [the longest x1 525 us: spread(): return lax.psum(kept, axis)]
    ppermute x10 -> x0, waiting for transfers between devices: 110 us -> none  [passed_along(): return lax.ppermute(x, axis, [(i, (i + by) % peers) for i in range(peers)])]
    pallas_call x0 -> x2, Pallas kernels: none -> 102 us  [the longest x1 99.8 us: local(): pl.pallas_call(layer_kernel, out_shape=results, in_specs=anywhere(6), out...]
    ppermute x10 -> x0, starting transfers between devices: 33 us -> none  [passed_along(): return lax.ppermute(x, axis, [(i, (i + by) % peers) for i in range(peers)])]
    dot_general x15 -> x0, matrix products: 31.6 us -> none  [the longest x1 6.09 us: local(): lax.dot_general(grad_full, mixed, (((0,), (0,)), ((), ())), preferred_ele...]
    another operation x8 -> x0, local copies, waits for them, and re-layouts: 18.7 us -> none  [the longest x4 15.1 us: local(): jnp.stack([band_dk.reshape(band_count, tok_dev, features), band_dv.reshap...]
    unnamed x55 -> x1, local copies, waits for them, and re-layouts: 18 us -> 1.42 us
  transfers between devices with their start and end apart: 16 -> 0, of which waited for: 11 -> 0; matrix products, arithmetic and copies ran while one was open for 5% -> 0% of each run, Pallas kernels for 0% -> 0%
where the time goes in v2:
time: 104 us
  Pallas kernels  102 us (98%)
  local copies, waits for them, and re-layouts  1.42 us (1%)
    pallas_call x1, Pallas kernels, local(): pl.pallas_call(layer_kernel, out_shape=results, in_specs=anywhere(6), out...  99.8 us
    pallas_call x1, Pallas kernels, local(): pl.pallas_call(hand_over_kernel, out_shape=results, in_specs=anywhere(5),...  2.22 us

profile of v2, /device:TPU:16, one launch (start us, length us, event | category | flops | bytes accessed | tf_op | source)
XLA Modules:
  0.0 104.1 jit_solution(15876811645078727066)
XLA Ops:
  0.6 1.4 %copy.11.lists_hbm = s32[128,3]{1,0:T(8,128)} copy(s32[128,3]{0,1:T(4,128)} %param.10) | data formatting | bytes 3072 | tf_op args[4]
  2.0 99.8 %layer.1 = (bf16[256,1024]{1,0:T(8,128)(2,1)}, bf16[256,512]{1,0:T(8,128)(2,1)}, bf16[256,512]{1,0:T(8,128)(2,1)}, bf16[256,512]{1,0:T(8,128)(2,1)}, f32[64,512]{1,0:T(8,128)}) custom-call(bf16[256,512]{1,0:T(8,128)(2,1)} %q.1, bf16[256,512]{1,0:T(8,128)(2,1)} %k.1, bf16[256,512]{1,0:T(8,128)(2,1)} %v.1, bf16[64,512]{1,0:T(8,128)(2,1)} %w.1, ...), custom_call_target="tpu_custom_call" | custom-call | tf_op jit(solution)/shard_map/layer/pallas_call | solution.py:700
  101.8 2.2 %hand_over.1 = (bf16[256,1024]{1,0:T(8,128)(2,1)}, bf16[256,512]{1,0:T(8,128)(2,1)}, bf16[256,512]{1,0:T(8,128)(2,1)}, bf16[256,512]{1,0:T(8,128)(2,1)}, f32[64,512]{1,0:T(8,128)}) custom-call(bf16[256,1024]{1,0:T(8,128)(2,1)} %get-tuple-element.10.refs_0_, bf16[256,512]{1,0:T(8,128)(2,1)} %get-tuple-element.11.refs_1_, ...), custom_call_target="tpu_custom_call" | custom-call | tf_op jit(solution)/shard_map/hand_over/pallas_call | solution.py:711

commit v3 on v2

v3 whole, which is shorter than its diff:
```python
import jax
import jax.numpy as jnp
from jax import lax
from jax.experimental import pallas as pl
from jax.experimental.pallas import tpu as pltpu
from jax.sharding import PartitionSpec as P

HD = 128
BLK = 128
SCALE = HD ** -0.5
BF = jnp.bfloat16
F32 = jnp.float32
NX, NZ, NY = 4, 8, 4
N_COPIES = 240


def place():
    i = lax.axis_index("ctx")
    h = lax.axis_index("head")
    cell = i // 2
    return cell // NZ, cell % NZ, (h // 2) * 2 + i % 2, h % 2, cell


def device(x, z, y, core):
    return ((x * NZ + z) * 2 + y % 2, (y // 2) * 2 + core)


def rows(start, size):
    return pl.ds(pl.multiple_of(start, size), size)


class Copies:
    def __init__(self, send, recv):
        self.send, self.recv, self.count = send, recv, 0

    def make(self, src, dst, target):
        k = self.count
        self.count += 1
        return pltpu.make_async_remote_copy(
            src_ref=src,
            dst_ref=dst,
            send_sem=self.send.at[k],
            recv_sem=self.recv.at[k],
            device_id=target,
            device_id_type=pl.DeviceIdType.MESH,
        )

    def start(self, src, dst, target):
        c = self.make(src, dst, target)
        c.start()
        return c


def greet(peers):
    barrier = pltpu.get_barrier_semaphore()
    for peer in peers:
        pl.semaphore_signal(
            barrier, inc=1, device_id=peer, device_id_type=pl.DeviceIdType.MESH
        )
    pl.semaphore_wait(barrier, len(peers))


def all_peers(x, z, y, core, cell):
    up, down = (cell + 1) % (NX * NZ), (cell + NX * NZ - 1) % (NX * NZ)
    peers = [device((x + d) % NX, z, y, core) for d in range(1, NX)]
    peers += [device(x, (z + d) % NZ, y, core) for d in range(1, NZ)]
    peers += [device(x, z, (y + d) % NY, core) for d in (1, NY - 1)]
    peers += [device(x, z, y, 1 - core)]
    peers += [device(c // NZ, c % NZ, y, core) for c in (up, down)]
    return peers


def dot(a, b, dims=(((1,), (0,)), ((), ()))):
    return lax.dot_general(a, b, dims, preferred_element_type=F32)


NT = (((1,), (1,)), ((), ()))
TN = (((0,), (0,)), ((), ()))


def add(dst, *srcs):
    n, lanes = dst.shape
    step = min(n, 16384 // lanes)

    def body(i, carry):
        r = rows(step * i, step)
        total = srcs[0][r, :].astype(F32)
        for s in srcs[1:]:
            total = total + s[r, :].astype(F32)
        dst[r, :] = total.astype(dst.dtype)
        return carry

    lax.fori_loop(0, n // step, body, 0)


def layer_kernel(
    q, k, v, w, lists_hbm, og,
    o_at, o_dq, o_dk, o_dv, o_wg,
    lists, q2, kb, vb, b0, wf, ogf, at, wg, probs, mixed, mgrad, dk, dv, d0, dq,
    at_core, at_sum, at_r1, at_r2, at_o, wg_r1, wg_s, wg_r2, wg_x, wz_s, wz_r, w_out,
    dke, dk_r, d0_b, d0_xr, d0_s, d0_zr, d0_t, d0_q, dkv_s, d_out, send, recv, lsem,
):
    x, z, y, core, cell = place()
    ylo = y % 2
    h = (y // 2) * 2 + core
    x_up, x_dn, x_far = (x + 1) % NX, (x + NX - 1) % NX, (x + 2) % NX
    z_up, z_dn = (z + 1) % NZ, (z + NZ - 1) % NZ
    c_up, c_dn = (cell + 1) % (NX * NZ), (cell + NX * NZ - 1) % (NX * NZ)
    y_mate = y + 1 - 2 * ylo
    y_next = (y + NY - 1 + 2 * ylo) % NY
    y_far = (y + 2) % NY
    mate, nxt = device(x, z, y_mate, core), device(x, z, y_next, core)
    twin = device(x, z, y, 1 - core)
    xu, xd = device(x_up, z, y, core), device(x_dn, z, y, core)
    zu, zd = device(x, z_up, y, core), device(x, z_dn, y, core)
    cu, cd = device(c_up // NZ, c_up % NZ, y, core), device(c_dn // NZ, c_dn % NZ, y, core)
    net = Copies(send, recv)
    mine, other = rows(256 * ylo, 256), rows(256 * (1 - ylo), 256)
    band_mine, band_other = rows(512 + 256 * ylo, 256), rows(512 + 256 * (1 - ylo), 256)
    lo_mine, lo_other = mine, other
    hi_mine, hi_other = rows(1024 + 256 * ylo, 256), rows(1024 + 256 * (1 - ylo), 256)
    ends, n_local = [], [0]

    def go(src, dst, target):
        c = net.start(src, dst, target)
        ends.append(c)
        return c

    def here(src, dst):
        c = pltpu.make_async_copy(src, dst, lsem.at[n_local[0]])
        n_local[0] += 1
        return c

    def here_now(src, dst):
        c = here(src, dst)
        c.start()
        return c

    w_loc = here_now(w.at[:, mine], wf.at[x, z, rows(64 * ylo, 64), :])
    k_loc = here_now(k.at[:, mine], kb.at[band_mine, :])
    v_loc = here_now(v.at[:, mine], vb.at[band_mine, :])
    og_loc = here_now(og, ogf.at[ylo, h])
    q_loc = here_now(q.at[:, mine], q2.at[mine, :])
    list_loc = here_now(lists_hbm, lists)
    greet(all_peers(x, z, y, core, cell))

    quarter = rows(64 * x, 64)
    b_mate = [
        net.make(k.at[0:BLK, other], b0.at[0:BLK, :], mate),
        net.make(v.at[0:BLK, other], b0.at[BLK : 2 * BLK, :], mate),
    ]
    b_loc = [
        here(k.at[0:BLK, mine], b0.at[0:BLK, :]),
        here(v.at[0:BLK, mine], b0.at[BLK : 2 * BLK, :]),
    ]
    b_to_x = [
        net.make(
            b0.at[rows(64 * ((x + d) % NX), 64), :],
            b0.at[rows(64 * ((x + d) % NX), 64), :],
            device((x + d) % NX, z, y, core),
        )
        for d in range(1, NX)
    ]
    b_along_z = [
        net.make(b0.at[quarter, :], b0.at[quarter, :], device(x, (z + d) % NZ, y, core))
        for d in range(1, NZ)
    ]

    @pl.when((cell == 0) & (ylo == 0))
    def _():
        for c in b_mate + b_loc:
            c.start()

    w_mate = go(w.at[:, other], wf.at[x, z, rows(64 * ylo, 64), :], mate)
    k_mate = go(k.at[:, other], kb.at[band_mine, :], mate)
    v_mate = go(v.at[:, other], vb.at[band_mine, :], mate)
    og_next = go(og, ogf.at[ylo, h], nxt)
    half, cut = 112, 224
    og_here = ogf.at[ylo, h]
    og_mate = [go(og.at[0:half, :], og_here.at[0:half, :], mate)]
    q_mate = go(q.at[:, other], q2.at[mine, :], mate)
    og_mate.append(go(og.at[half:256, :], og_here.at[half:256, :], mate))
    og_tw = [go(og, og_here, twin)]

    own_half, mate_half = rows(64 * ylo, 64), rows(64 * (1 - ylo), 64)
    first = [go(w.at[:, mine], wf.at[x, z, own_half, :], t) for t in (zu, zd, xu, xd)]
    halo = [
        go(k.at[:, mine], kb.at[lo_mine, :], cu),
        go(k.at[:, mine], kb.at[hi_mine, :], cd),
    ]
    w_mate.wait_recv()
    w_loc.wait()

    x_plus, x_minus, x_fwd = {}, {}, []

    def to_x(off):
        zz = (z + off) % NZ
        x_plus[off] = go(wf.at[x, zz], wf.at[x, zz], xu)
        x_minus[off] = go(wf.at[x, zz], wf.at[x, zz], xd)

    def either(cond, fn, then, other):
        @pl.when(cond)
        def _():
            fn(then)

        @pl.when(jnp.logical_not(cond))
        def _():
            fn(other)

    def goes_up(is_up):
        return (z == 7) | (z != 0) if is_up else z == 7

    def pass_x(off):
        zz = (z + off) % NZ
        if off == 0:
            first[2].wait_recv()
            first[3].wait_recv()
        x_plus[off].wait_recv()
        x_minus[off].wait_recv()
        pair = (
            goes_up(off in (0, 6, 2, 4)),
            net.make(wf.at[x_dn, zz], wf.at[x_dn, zz], xu),
            net.make(wf.at[x_up, zz], wf.at[x_up, zz], xd),
        )
        either(pair[0], lambda c: c.start(), pair[1], pair[2])
        x_fwd.append(pair)

    def ring_step(s, up, dn):
        zm, zp = (z + NZ - s) % NZ, (z + s) % NZ
        if s == 1:
            first[0].wait_recv()
            first[1].wait_recv()
        up.wait_recv()
        if s < 3:
            up = go(wf.at[x, zm], wf.at[x, zm], zu)
        else:
            up = go(wf.at[x, zm, 0:64, :], wf.at[x, zm, 0:64, :], zu)
        to_x(NZ - s)
        dn.wait_recv()
        if s < 3:
            dn = go(wf.at[x, zp], wf.at[x, zp], zd)
        else:
            dn = go(wf.at[x, zp, 64:128, :], wf.at[x, zp, 64:128, :], zd)
        to_x(s)
        return up, dn

    second = wf.at[x, z, mate_half, :]
    up = go(second, second, zu)
    dn = go(second, second, zd)
    x_plus[0] = go(second, second, xu)
    x_minus[0] = go(second, second, xd)

    @pl.when(cell == 0)
    def _():
        @pl.when(ylo == 0)
        def _():
            for c in b_loc:
                c.wait()

        @pl.when(ylo == 1)
        def _():
            for c in b_mate:
                c.wait_recv()

        for c in b_to_x:
            c.start()

    up, dn = ring_step(1, up, dn)
    halo += [
        go(v.at[:, mine], vb.at[lo_mine, :], cu),
        go(v.at[:, mine], vb.at[hi_mine, :], cd),
    ]

    @pl.when(z == 0)
    def _():
        for d in range(1, NX):

            @pl.when(x == d)
            def _():
                b_to_x[d - 1].wait_recv()

        for n in (3, 4, 2, 5, 1, 6, 0):
            b_along_z[n].start()

    k_mate.wait_recv()
    k_loc.wait()
    up, dn = ring_step(2, up, dn)
    halo += [
        go(kb.at[band_other, :], kb.at[lo_other, :], cu),
        go(kb.at[band_other, :], kb.at[hi_other, :], cd),
    ]
    pass_x(0)
    v_mate.wait_recv()
    v_loc.wait()
    up, dn = ring_step(3, up, dn)
    halo += [
        go(vb.at[band_other, :], vb.at[lo_other, :], cu),
        go(vb.at[band_other, :], vb.at[hi_other, :], cd),
    ]
    for d in range(1, NZ):

        @pl.when(z == d)
        def _():
            b_along_z[d - 1].wait_recv()

    b_along_x = [
        net.make(b0.at[quarter, :], b0.at[quarter, :], device((x + d) % NX, z, y, core))
        for d in range(1, NX)
    ]

    def to_x_peers(fn):
        for d in range(1, NX):

            @pl.when((z != 0) | ((x + d) % NX != 0))
            def _():
                fn(b_along_x[d - 1])

    to_x_peers(lambda c: c.start())

    from_mate = ogf.at[y_mate % 2, (y_mate // 2) * 2 + core]
    from_next = ogf.at[y_next % 2, (y_next // 2) * 2 + core]
    far = ogf.at[y_far % 2, (y_far // 2) * 2 + core]
    og_mate[0].wait_recv()
    fwd_next = [go(from_mate.at[0:half, :], from_mate.at[0:half, :], nxt)]
    og_tw.append(go(from_mate.at[0:half, :], from_mate.at[0:half, :], twin))
    og_next.wait_recv()
    fwd_mate = go(from_next.at[cut:256, :], from_next.at[cut:256, :], mate)
    og_tw.append(go(from_next, from_next, twin))
    pass_x(7)
    pass_x(1)
    up.wait_recv()
    dn.wait_recv()
    to_x(4)
    pass_x(6)
    pass_x(2)
    q_mate.wait_recv()
    q_loc.wait()
    list_loc.wait()

    @pl.when(cell != 0)
    def _():
        for d in range(1, NX):
            b_along_x[d - 1].wait_recv()

    for c in halo:
        c.wait_recv()

    def window(n):
        i, head = n % 4, n // 4
        return i, head, rows(128 * i, 128), pl.ds(pl.multiple_of(128 * i, 128), 1152), rows(128 * head, 128)

    def forward(n, carry):
        i, head, toks, win, lanes = window(n)
        b = 4 * cell + i
        bias = []
        for j in range(9):
            kbl = b - 4 + j
            good = (kbl >= 1) & (kbl <= 127)
            if j not in (3, 4, 5):
                named = (lists[0, b] == kbl) | (lists[1, b] == kbl) | (lists[2, b] == kbl)
                good = good & named
            bias.append(jnp.full((1, BLK), jnp.where(good, 0.0, -jnp.inf), F32))
        bias = jnp.concatenate(bias, axis=1)
        qq = q2[toks, lanes]
        s0 = dot(qq, b0[0:BLK, lanes], NT) * SCALE
        s1 = dot(qq, kb[win, lanes], NT) * SCALE + bias
        top = jnp.maximum(jnp.max(s0, axis=1, keepdims=True), jnp.max(s1, axis=1, keepdims=True))
        e0, e1 = jnp.exp(s0 - top), jnp.exp(s1 - top)
        inv = 1.0 / (jnp.sum(e0, axis=1, keepdims=True) + jnp.sum(e1, axis=1, keepdims=True))
        p0, p1 = e0 * inv, e1 * inv
        probs[n, :, 0:BLK] = p0
        probs[n, :, BLK:] = p1
        out = dot(p0.astype(BF), b0[BLK : 2 * BLK, lanes]) + dot(p1.astype(BF), vb[win, lanes])
        mixed[toks, lanes] = out.astype(BF)
        return carry

    og_mate[1].wait_recv()
    fwd_next.append(go(from_mate.at[half:cut, :], from_mate.at[half:cut, :], nxt))
    og_tw.append(go(from_mate.at[half:256, :], from_mate.at[half:256, :], twin))
    lax.fori_loop(0, 2, forward, 0)
    pass_x(5)
    pass_x(3)
    lax.fori_loop(2, 4, forward, 0)
    pass_x(4)
    lax.fori_loop(4, 5, forward, 0)
    fwd_mate.wait_recv()
    og_tw.append(go(far.at[cut:256, :], far.at[cut:256, :], twin))
    fwd_next[0].wait_recv()
    og_tw.append(go(far.at[0:half, :], far.at[0:half, :], twin))
    lax.fori_loop(5, 8, forward, 0)
    fwd_next[1].wait_recv()
    og_tw.append(go(far.at[half:cut, :], far.at[half:cut, :], twin))
    og_loc.wait()
    for c in og_tw:
        c.wait_recv()

    def weight_part(xx):
        total = dot(mixed[0:256, :], ogf[0, xx], TN) + dot(mixed[256:512, :], ogf[1, xx], TN)
        for n in range(8):
            wg[xx, n] = total[:, 128 * n : 128 * (n + 1)].astype(BF)

    def attended_part(t, c):
        hh = (t // 2) * 2 + c
        part = dot(mixed[rows(256 * (t % 2), 256), :], wf[hh].reshape(1024, 256), NT)
        at[t % 2, hh] = part.astype(BF)

    w1, w2u, w2d = {}, {}, {}

    def piece(xx, off):
        return wg.at[xx, (z + off) % NZ]

    def straight(off):
        if off < 4:
            w2u[off] = go(piece(x_up, off), wg_r2.at[0, off], xu)
        else:
            w2d[off] = go(piece(x_dn, off), wg_r2.at[1, off], xd)

    def relay(off):
        w1[off].wait_recv()
        if off >= 4:
            add(wg_s.at[off], piece(x_up, off), wg_r1.at[off])
            w2u[off] = go(wg_s.at[off], wg_r2.at[0, off], xu)
        else:
            add(wg_s.at[off], piece(x_dn, off), wg_r1.at[off])
            w2d[off] = go(wg_s.at[off], wg_r2.at[1, off], xd)

    weight_part(x_far)
    for off in (4, 3, 5, 2, 6, 1, 7, 0):
        w1[off] = go(piece(x_far, off), wg_r1.at[off], xu if off >= 4 else xd)
    for pair in x_fwd:
        either(pair[0], lambda c: c.wait_recv(), pair[1], pair[2])
    order = (y_far, y_mate, y_next, y)
    cores = []
    for t in order:
        attended_part(t, 1 - core)
        cores.append(go(at.at[t % 2, (t // 2) * 2 + 1 - core], at_core.at[t], twin))
    weight_part(x_up)
    weight_part(x_dn)
    for off in (4, 3, 5, 2):
        straight(off)
    for t in order:
        attended_part(t, core)
    weight_part(x)
    for t in range(2):
        total = jnp.zeros((256, 256), F32)
        for hh in range(4):
            total = total + dot(ogf[t, hh], wf[hh].reshape(1024, 256))
        mgrad[256 * t : 256 * (t + 1), :] = total.astype(BF)
    dk[...] = jnp.zeros_like(dk)
    dv[...] = jnp.zeros_like(dv)
    d0[...] = jnp.zeros_like(d0)
    for off in (4, 3, 5, 2):
        relay(off)
    for off in (6, 1, 7, 0):
        straight(off)

    for n, t in enumerate(order):
        cores[n].wait_recv()
        add(at_sum.at[t], at.at[t % 2, (t // 2) * 2 + core], at_core.at[t])
        if n == 0:
            a1n = go(at_sum.at[t, 0:128, :], at_r1.at[0], nxt)
            a1m = go(at_sum.at[t, 128:256, :], at_r1.at[1], mate)
        if n == 1:
            a2m = [go(at_sum.at[t, 128:256, :], at_r2.at[0, 128:256, :], mate)]
        if n == 2:
            a2n = [go(at_sum.at[t, 0:128, :], at_r2.at[1, 0:128, :], nxt)]

    def backward(n, carry):
        i, head, toks, win, lanes = window(n)
        g = mgrad[toks, lanes]
        delta = jnp.sum(
            g.astype(F32) * mixed[toks, lanes].astype(F32), axis=1, keepdims=True
        )
        p0, p1 = probs[n, :, 0:BLK], probs[n, :, BLK:]
        sl0 = (p0 * (dot(g, b0[BLK : 2 * BLK, lanes], NT) - delta)).astype(BF)
        sl1 = (p1 * (dot(g, vb[win, lanes], NT) - delta)).astype(BF)
        out = dot(sl0, b0[0:BLK, lanes]) + dot(sl1, kb[win, lanes])
        dq[toks, lanes] = (out * SCALE).astype(BF)
        qq = q2[toks, lanes]
        dk[win, lanes] += dot(sl1, qq, TN)
        dv[win, lanes] += dot(p1.astype(BF), g, TN)
        d0[0, :, lanes] += dot(sl0, qq, TN)
        d0[1, :, lanes] += dot(p0.astype(BF), g, TN)
        return carry

    edges, q_out, locals_out = [[], []], [], []

    def leave(head, n):
        acc, factor = ((dk, SCALE), (dv, 1.0))[n]
        lanes = slice(128 * head, 128 * (head + 1))
        dke[head, n, 0] = (acc[0:512, lanes] * factor).astype(BF)
        dke[head, n, 1] = (acc[1024:1536, lanes] * factor).astype(BF)
        edges[head] += [
            go(dke.at[head, n, 0], dk_r.at[head, n, 1], cd),
            go(dke.at[head, n, 1], dk_r.at[head, n, 0], cu),
        ]

    def leave_q(head):
        lanes = slice(128 * head, 128 * (head + 1))
        cols = rows(256 * ylo + 128 * head, 128)
        q_out.append(go(dq.at[other, lanes], o_dq.at[:, cols], mate))
        locals_out.append(here_now(dq.at[mine, lanes], o_dq.at[:, cols]))

    def sum_x(off):
        w2u[off].wait_recv()
        w2d[off].wait_recv()
        add(wg_x.at[off], piece(x, off), wg_r2.at[0, off], wg_r2.at[1, off])

    def z_step(s, up, dn):
        tu, td = 5 - s, 3 + s
        up.wait_recv()
        if s == 2:
            add(wz_s.at[0, 1, 0:128, :], wg_x.at[tu, 0:128, :], wz_r.at[0, 0, 0:128, :])
            add(wz_s.at[0, 1, 128:256, :], wg_x.at[tu, 128:256, :])
        else:
            add(wz_s.at[0, s - 1], wg_x.at[tu], wz_r.at[0, s - 2])
        up = go(wz_s.at[0, s - 1], wz_r.at[0, s - 1], zu)
        dn.wait_recv()
        if s == 2:
            add(wz_s.at[1, 1, 128:256, :], wg_x.at[td, 128:256, :], wz_r.at[1, 0, 128:256, :])
            add(wz_s.at[1, 1, 0:128, :], wg_x.at[td, 0:128, :])
        else:
            add(wz_s.at[1, s - 1], wg_x.at[td], wz_r.at[1, s - 2])
        dn = go(wz_s.at[1, s - 1], wz_r.at[1, s - 1], zd)
        return up, dn

    lax.fori_loop(0, 4, backward, 0)
    for off in (6, 1, 7, 0):
        relay(off)
    leave(0, 0)
    leave_q(0)
    lax.fori_loop(4, 8, backward, 0)

    d0_b[0:BLK, :] = (d0[0] * SCALE).astype(BF)
    d0_b[BLK : 2 * BLK, :] = d0[1].astype(BF)
    d0_x = [
        go(
            d0_b.at[rows(64 * ((x + d) % NX), 64), :],
            d0_xr.at[d - 1],
            device((x + d) % NX, z, y, core),
        )
        for d in range(1, NX)
    ]
    d0_z = [net.make(d0_s, d0_zr.at[d - 1], device(x, 0, y, core)) for d in range(1, NZ)]
    d0_o = [net.make(d0_t, d0_q.at[d - 1], device(0, z, y, core)) for d in range(1, NX)]

    sum_x(4)
    add(wz_s.at[0, 0, 0:128, :], wg_x.at[4, 0:128, :])
    up = go(wz_s.at[0, 0, 0:128, :], wz_r.at[0, 0, 0:128, :], zu)
    add(wz_s.at[1, 0, 128:256, :], wg_x.at[4, 128:256, :])
    dn = go(wz_s.at[1, 0, 128:256, :], wz_r.at[1, 0, 128:256, :], zd)
    leave(0, 1)
    leave_q(1)
    sum_x(3)
    sum_x(5)
    up, dn = z_step(2, up, dn)
    leave(1, 0)

    a1n.wait_recv()
    to_mate = at_core.at[0, 0:128, :]
    add(to_mate, at_sum.at[y_mate, 0:128, :], at_r1.at[0])
    a2m.append(go(to_mate, at_r2.at[0, 0:128, :], mate))
    a1m.wait_recv()
    to_next = at_core.at[1, 128:256, :]
    add(to_next, at_sum.at[y_next, 128:256, :], at_r1.at[1])
    a2n.append(go(to_next, at_r2.at[1, 128:256, :], nxt))

    sum_x(2)
    sum_x(6)
    up, dn = z_step(3, up, dn)
    leave(1, 1)

    for c in d0_x:
        c.wait_recv()
    add(d0_s, d0_b.at[quarter, :], *[d0_xr.at[d] for d in range(3)])
    for d in range(1, NZ):

        @pl.when(z == d)
        def _():
            d0_z[d - 1].start()

    kv_mate, kv_here = [[], []], [[], []]

    def finish(head):
        for c in edges[head]:
            c.wait_recv()
        lanes = slice(128 * head, 128 * (head + 1))
        cols = rows(256 * ylo + 128 * head, 128)
        for n, (acc, factor) in enumerate(((dk, SCALE), (dv, 1.0))):
            dkv_s[n, :, lanes] = (
                acc[512:1024, lanes] * factor
                + dk_r[head, n, 0].astype(F32)
                + dk_r[head, n, 1].astype(F32)
            )
            out = (o_dk, o_dv)[n]
            for r in (0, BLK):
                src = d_out.at[n, rows(256 * (1 - ylo) + r, BLK), lanes]
                kv_mate[head].append(net.make(src, out.at[r : r + BLK, cols], mate))
            kv_here[head].append(here(d_out.at[n, mine, lanes], out.at[:, cols]))

        d_out[:, :, lanes] = dkv_s[:, :, lanes].astype(BF)
        for m, c in enumerate(kv_mate[head]):
            if m % 2 == 1:
                c.start()
            else:
                pl.when((cell != 0) | (ylo == 0))(c.start)
        for c in kv_here[head]:
            pl.when(cell != 0)(c.start)

    finish(0)
    sum_x(1)
    sum_x(7)
    up, dn = z_step(4, up, dn)

    @pl.when(z == 0)
    def _():
        for c in d0_z:
            c.wait_recv()
        add(d0_t, d0_s, *[d0_zr.at[d] for d in range(NZ - 1)])
        for d in range(1, NX):

            @pl.when(x == d)
            def _():
                d0_o[d - 1].start()

    finish(1)
    sum_x(0)
    up.wait_recv()
    dn.wait_recv()
    add(wg_x.at[0], wg_x.at[0], wz_r.at[0, 3], wz_r.at[1, 3])
    w_out[...] = wg_x[0].T
    w_last = go(w_out.at[rows(64 * (1 - ylo), 64), :], o_wg.at[:, mine], mate)
    locals_out.append(here_now(w_out.at[rows(64 * ylo, 64), :], o_wg.at[:, mine]))

    @pl.when(cell == 0)
    def _():
        for c in d0_o:
            c.wait_recv()
        for m in range(4):
            part = d0_t[...] if m == 0 else d0_q[m - 1]
            dkv_s[m // 2, 64 * (m % 2) : 64 * (m % 2) + 64, :] += part.astype(F32)
        d_out[:, 0:BLK, :] = dkv_s[:, 0:BLK, :].astype(BF)

        @pl.when(ylo == 1)
        def _():
            for head in range(2):
                for c in kv_mate[head][0::2]:
                    c.start()

        for c in kv_here[0] + kv_here[1]:
            c.start()

    for c in a2m + a2n:
        c.wait_recv()
    add(at_o, at_sum.at[y], at_r2.at[0], at_r2.at[1])
    locals_out.append(here_now(at_o, o_at))

    for c in kv_mate[0] + kv_mate[1] + q_out + [w_last]:
        c.wait_recv()
    for c in locals_out + kv_here[0] + kv_here[1]:
        c.wait()
    for c in ends + kv_mate[0] + kv_mate[1]:
        c.wait_send()
    for pair in x_fwd:
        either(pair[0], lambda c: c.wait_send(), pair[1], pair[2])

    @pl.when(cell == 0)
    def _():
        @pl.when(ylo == 0)
        def _():
            for c in b_mate:
                c.wait_send()

        for c in b_to_x:
            c.wait_send()

    to_x_peers(lambda c: c.wait_send())

    @pl.when(z == 0)
    def _():
        for c in b_along_z:
            c.wait_send()

        for d in range(1, NX):

            @pl.when(x == d)
            def _():
                d0_o[d - 1].wait_send()

    for d in range(1, NZ):

        @pl.when(z == d)
        def _():
            d0_z[d - 1].wait_send()


def hand_over_kernel(*refs):
    n = 5
    ins, outs, bufs, sem = refs[:n], refs[n : 2 * n], refs[2 * n : 3 * n], refs[3 * n]
    reads = [pltpu.make_async_copy(ins[i], bufs[i], sem.at[0, i]) for i in range(n)]
    writes = [pltpu.make_async_copy(bufs[i], outs[i], sem.at[1, i]) for i in range(n)]
    for c in reads:
        c.start()
    for i in range(n):
        reads[i].wait()
        writes[i].start()
    for c in writes:
        c.wait()


def anywhere(n):
    return [pl.BlockSpec(memory_space=pl.ANY)] * n


def local(queries, key_heads, value_heads, out_weight, block_lists, out_grad):
    results = (
        jax.ShapeDtypeStruct((256, 1024), BF),
        jax.ShapeDtypeStruct((256, 512), BF),
        jax.ShapeDtypeStruct((256, 512), BF),
        jax.ShapeDtypeStruct((256, 512), BF),
        jax.ShapeDtypeStruct((64, 512), F32),
    )
    b, f = (lambda *s: pltpu.VMEM(s, BF)), (lambda *s: pltpu.VMEM(s, F32))
    scratch = [
        pltpu.SMEM((3, 128), jnp.int32),
        b(512, 256),
        b(1536, 256),
        b(1536, 256),
        b(256, 256),
        b(NX, NZ, 128, 256),
        b(2, 4, 256, 1024),
        b(2, 4, 256, 1024),
        b(4, 8, 256, 128),
        f(8, 128, 1280),
        b(512, 256),
        b(512, 256),
        f(1536, 256),
        f(1536, 256),
        f(2, 128, 256),
        b(512, 256),
        b(4, 256, 1024),
        b(4, 256, 1024),
        b(2, 128, 1024),
        b(2, 256, 1024),
        b(256, 1024),
        b(8, 256, 128),
        b(8, 256, 128),
        b(2, 8, 256, 128),
        f(8, 256, 128),
        b(2, 4, 256, 128),
        b(2, 4, 256, 128),
        f(128, 256),
        b(2, 2, 2, 512, 128),
        b(2, 2, 2, 512, 128),
        b(256, 256),
        b(3, 64, 256),
        b(64, 256),
        b(7, 64, 256),
        b(64, 256),
        b(3, 64, 256),
        f(2, 512, 256),
        b(2, 512, 256),
        pltpu.SemaphoreType.DMA((N_COPIES,)),
        pltpu.SemaphoreType.DMA((N_COPIES,)),
        pltpu.SemaphoreType.DMA((24,)),
    ]
    outs = pl.pallas_call(
        layer_kernel,
        out_shape=results,
        in_specs=anywhere(6),
        out_specs=tuple(anywhere(5)),
        scratch_shapes=scratch,
        compiler_params=pltpu.CompilerParams(
            collective_id=0, has_side_effects=True, vmem_limit_bytes=60 * 1024 * 1024
        ),
        name="layer",
    )(queries, key_heads, value_heads, out_weight, block_lists.T, out_grad)
    return pl.pallas_call(
        hand_over_kernel,
        out_shape=results,
        in_specs=anywhere(5),
        out_specs=tuple(anywhere(5)),
        scratch_shapes=[pltpu.VMEM(r.shape, r.dtype) for r in results]
        + [pltpu.SemaphoreType.DMA((2, 5))],
        name="hand_over",
    )(*outs)


def solution(mesh):
    placed = P("ctx", "head")
    return jax.shard_map(
        local,
        mesh=mesh,
        in_specs=(placed, placed, placed, placed, P(), placed),
        out_specs=(placed,) * 5,
        check_vma=False,
    )
```

time: 104 us -> 93 us (0.89); the launches traced: 104 us -> 91.1 us
  Pallas kernels: 102 us -> 90.5 us
  local copies, waits for them, and re-layouts: 1.42 us -> 0 us
    pallas_call x1, Pallas kernels: 99.8 us -> 88.3 us  [local(): pl.pallas_call(layer_kernel, out_shape=results, in_specs=anywhere(6), out...]
    unnamed x1 -> x0, local copies, waits for them, and re-layouts: 1.42 us -> none
where the time goes in v3:
time: 93 us; the launch traced here: 91.1 us
  Pallas kernels  90.5 us (97%)
    pallas_call x1, Pallas kernels, local(): pl.pallas_call(layer_kernel, out_shape=results, in_specs=anywhere(6), out...  88.3 us
    pallas_call x1, Pallas kernels, local(): pl.pallas_call(hand_over_kernel, out_shape=results, in_specs=anywhere(5),...  2.22 us

profile of v3, /device:TPU:16, one launch (start us, length us, event | category | flops | bytes accessed | tf_op | source)
XLA Modules:
  0.0 91.1 jit_solution(2734569115411145328)
XLA Ops:
  0.6 88.3 %layer.1 = (bf16[256,1024]{1,0:T(8,128)(2,1)}, bf16[256,512]{1,0:T(8,128)(2,1)}, bf16[256,512]{1,0:T(8,128)(2,1)}, bf16[256,512]{1,0:T(8,128)(2,1)}, f32[64,512]{1,0:T(8,128)}) custom-call(bf16[256,512]{1,0:T(8,128)(2,1)} %q.1, bf16[256,512]{1,0:T(8,128)(2,1)} %k.1, bf16[256,512]{1,0:T(8,128)(2,1)} %v.1, bf16[64,512]{1,0:T(8,128)(2,1)} %w.1, ...), custom_call_target="tpu_custom_call" | custom-call | tf_op jit(solution)/shard_map/layer/pallas_call | solution.py:767
  88.9 2.2 %hand_over.1 = (bf16[256,1024]{1,0:T(8,128)(2,1)}, bf16[256,512]{1,0:T(8,128)(2,1)}, bf16[256,512]{1,0:T(8,128)(2,1)}, bf16[256,512]{1,0:T(8,128)(2,1)}, f32[64,512]{1,0:T(8,128)}) custom-call(bf16[256,1024]{1,0:T(8,128)(2,1)} %get-tuple-element.10.refs_0_, bf16[256,512]{1,0:T(8,128)(2,1)} %get-tuple-element.11.refs_1_, ...), custom_call_target="tpu_custom_call" | custom-call | tf_op jit(solution)/shard_map/hand_over/pallas_call | solution.py:778

commit v4 on v3

--- a/solution.py
+++ b/solution.py
@@ -11,7 +11,8 @@
 BF = jnp.bfloat16
 F32 = jnp.float32
 NX, NZ, NY = 4, 8, 4
-N_COPIES = 240
+POOL = 40
+COUNTS = N_SEND, N_RECV, N_LOCAL = 106, 150, 16
 
 
 def place():
@@ -31,24 +32,39 @@
 
 class Copies:
     def __init__(self, send, recv):
-        self.send, self.recv, self.count = send, recv, 0
-
-    def make(self, src, dst, target):
-        k = self.count
-        self.count += 1
+        self.send, self.recv = send, recv
+        self.n_send, self.n_recv, self.live = POOL, 0, []
+
+    def numbers(self):
+        self.n_send += 1
+        self.n_recv += 1
+        return self.n_send - 1, self.n_recv - 1
+
+    def make(self, src, dst, target, numbers=None):
+        k_send, k_recv = numbers or self.numbers()
         return pltpu.make_async_remote_copy(
             src_ref=src,
             dst_ref=dst,
-            send_sem=self.send.at[k],
-            recv_sem=self.recv.at[k],
+            send_sem=self.send.at[k_send],
+            recv_sem=self.recv.at[k_recv],
             device_id=target,
             device_id_type=pl.DeviceIdType.MESH,
         )
 
     def start(self, src, dst, target):
-        c = self.make(src, dst, target)
+        k_send = len(self.live)
+        if k_send == POOL:
+            k_send, oldest = self.live.pop(0)
+            oldest.wait_send()
+        self.n_recv += 1
+        c = self.make(src, dst, target, (k_send, self.n_recv - 1))
         c.start()
+        self.live.append((k_send, c))
         return c
+
+    def drain(self):
+        for _, c in self.live:
+            c.wait_send()
 
 
 def greet(peers):
@@ -119,12 +135,10 @@
     band_mine, band_other = rows(512 + 256 * ylo, 256), rows(512 + 256 * (1 - ylo), 256)
     lo_mine, lo_other = mine, other
     hi_mine, hi_other = rows(1024 + 256 * ylo, 256), rows(1024 + 256 * (1 - ylo), 256)
-    ends, n_local = [], [0]
+    n_local = [0]
 
     def go(src, dst, target):
-        c = net.start(src, dst, target)
-        ends.append(c)
-        return c
+        return net.start(src, dst, target)
 
     def here(src, dst):
         c = pltpu.make_async_copy(src, dst, lsem.at[n_local[0]])
@@ -175,7 +189,7 @@
     k_mate = go(k.at[:, other], kb.at[band_mine, :], mate)
     v_mate = go(v.at[:, other], vb.at[band_mine, :], mate)
     og_next = go(og, ogf.at[ylo, h], nxt)
-    half, cut = 112, 224
+    half, cut = 160, 208
     og_here = ogf.at[ylo, h]
     og_mate = [go(og.at[0:half, :], og_here.at[0:half, :], mate)]
     q_mate = go(q.at[:, other], q2.at[mine, :], mate)
@@ -217,10 +231,11 @@
             first[3].wait_recv()
         x_plus[off].wait_recv()
         x_minus[off].wait_recv()
+        ks = net.numbers()
         pair = (
             goes_up(off in (0, 6, 2, 4)),
-            net.make(wf.at[x_dn, zz], wf.at[x_dn, zz], xu),
-            net.make(wf.at[x_up, zz], wf.at[x_up, zz], xd),
+            net.make(wf.at[x_dn, zz], wf.at[x_dn, zz], xu, ks),
+            net.make(wf.at[x_up, zz], wf.at[x_up, zz], xd, ks),
         )
         either(pair[0], lambda c: c.start(), pair[1], pair[2])
         x_fwd.append(pair)
@@ -266,22 +281,22 @@
             c.start()
 
     up, dn = ring_step(1, up, dn)
+
+    @pl.when(z == 0)
+    def _():
+        for d in range(1, NX):
+
+            @pl.when(x == d)
+            def _():
+                b_to_x[d - 1].wait_recv()
+
+        for n in (3, 4, 2, 5, 1, 6, 0):
+            b_along_z[n].start()
+
     halo += [
         go(v.at[:, mine], vb.at[lo_mine, :], cu),
         go(v.at[:, mine], vb.at[hi_mine, :], cd),
     ]
-
-    @pl.when(z == 0)
-    def _():
-        for d in range(1, NX):
-
-            @pl.when(x == d)
-            def _():
-                b_to_x[d - 1].wait_recv()
-
-        for n in (3, 4, 2, 5, 1, 6, 0):
-            b_along_z[n].start()
-
     k_mate.wait_recv()
     k_loc.wait()
     up, dn = ring_step(2, up, dn)
@@ -290,6 +305,26 @@
         go(kb.at[band_other, :], kb.at[hi_other, :], cd),
     ]
     pass_x(0)
+    for d in range(1, NZ):
+
+        @pl.when(z == d)
+        def _():
+            b_along_z[d - 1].wait_recv()
+
+    b_along_x = [
+        net.make(b0.at[quarter, :], b0.at[quarter, :], device((x + d) % NX, z, y, core))
+        for d in range(1, NX)
+    ]
+
+    def to_x_peers(fn):
+        for d in range(1, NX):
+
+            @pl.when((z != 0) | ((x + d) % NX != 0))
+            def _():
+                fn(b_along_x[d - 1])
+
+    to_x_peers(lambda c: c.start())
+
     v_mate.wait_recv()
     v_loc.wait()
     up, dn = ring_step(3, up, dn)
@@ -297,26 +332,6 @@
         go(vb.at[band_other, :], vb.at[lo_other, :], cu),
         go(vb.at[band_other, :], vb.at[hi_other, :], cd),
     ]
-    for d in range(1, NZ):
-
-        @pl.when(z == d)
-        def _():
-            b_along_z[d - 1].wait_recv()
-
-    b_along_x = [
-        net.make(b0.at[quarter, :], b0.at[quarter, :], device((x + d) % NX, z, y, core))
-        for d in range(1, NX)
-    ]
-
-    def to_x_peers(fn):
-        for d in range(1, NX):
-
-            @pl.when((z != 0) | ((x + d) % NX != 0))
-            def _():
-                fn(b_along_x[d - 1])
-
-    to_x_peers(lambda c: c.start())
-
     from_mate = ogf.at[y_mate % 2, (y_mate // 2) * 2 + core]
     from_next = ogf.at[y_next % 2, (y_next // 2) * 2 + core]
     far = ogf.at[y_far % 2, (y_far // 2) * 2 + core]
@@ -327,12 +342,10 @@
     fwd_mate = go(from_next.at[cut:256, :], from_next.at[cut:256, :], mate)
     og_tw.append(go(from_next, from_next, twin))
     pass_x(7)
-    pass_x(1)
     up.wait_recv()
     dn.wait_recv()
     to_x(4)
-    pass_x(6)
-    pass_x(2)
+    pass_x(1)
     q_mate.wait_recv()
     q_loc.wait()
     list_loc.wait()
@@ -374,15 +387,17 @@
         mixed[toks, lanes] = out.astype(BF)
         return carry
 
+    lax.fori_loop(0, 1, forward, 0)
+    pass_x(6)
     og_mate[1].wait_recv()
     fwd_next.append(go(from_mate.at[half:cut, :], from_mate.at[half:cut, :], nxt))
     og_tw.append(go(from_mate.at[half:256, :], from_mate.at[half:256, :], twin))
-    lax.fori_loop(0, 2, forward, 0)
+    pass_x(2)
+    lax.fori_loop(1, 3, forward, 0)
     pass_x(5)
     pass_x(3)
-    lax.fori_loop(2, 4, forward, 0)
+    lax.fori_loop(3, 5, forward, 0)
     pass_x(4)
-    lax.fori_loop(4, 5, forward, 0)
     fwd_mate.wait_recv()
     og_tw.append(go(far.at[cut:256, :], far.at[cut:256, :], twin))
     fwd_next[0].wait_recv()
@@ -409,24 +424,50 @@
     def piece(xx, off):
         return wg.at[xx, (z + off) % NZ]
 
+    first_group, second_group = (4, 3, 5, 2), (6, 1, 7, 0)
+    for off in first_group + second_group:
+        ks, ku, kd = net.numbers(), net.numbers(), net.numbers()
+        w1[off] = (
+            off >= 4 if off in first_group else goes_up(off >= 4),
+            net.make(piece(x_far, off), wg_r1.at[off], xu, ks),
+            net.make(piece(x_far, off), wg_r1.at[off], xd, ks),
+        )
+        w2u[off] = (
+            net.make(piece(x_up, off), wg_r2.at[0, off], xu, ku),
+            net.make(wg_s.at[off], wg_r2.at[0, off], xu, ku),
+        )
+        w2d[off] = (
+            net.make(piece(x_dn, off), wg_r2.at[1, off], xd, kd),
+            net.make(wg_s.at[off], wg_r2.at[1, off], xd, kd),
+        )
+
+    def either_way(off, up_way, down_way):
+        is_up = w1[off][0]
+        if isinstance(is_up, bool):
+            (up_way if is_up else down_way)()
+        else:
+            pl.when(is_up)(up_way)
+            pl.when(jnp.logical_not(is_up))(down_way)
+
     def straight(off):
-        if off < 4:
-            w2u[off] = go(piece(x_up, off), wg_r2.at[0, off], xu)
-        else:
-            w2d[off] = go(piece(x_dn, off), wg_r2.at[1, off], xd)
+        either_way(off, w2d[off][0].start, w2u[off][0].start)
 
     def relay(off):
-        w1[off].wait_recv()
-        if off >= 4:
+        def up_way():
+            w1[off][1].wait_recv()
             add(wg_s.at[off], piece(x_up, off), wg_r1.at[off])
-            w2u[off] = go(wg_s.at[off], wg_r2.at[0, off], xu)
-        else:
+            w2u[off][1].start()
+
+        def down_way():
+            w1[off][2].wait_recv()
             add(wg_s.at[off], piece(x_dn, off), wg_r1.at[off])
-            w2d[off] = go(wg_s.at[off], wg_r2.at[1, off], xd)
+            w2d[off][1].start()
+
+        either_way(off, up_way, down_way)
 
     weight_part(x_far)
-    for off in (4, 3, 5, 2, 6, 1, 7, 0):
-        w1[off] = go(piece(x_far, off), wg_r1.at[off], xu if off >= 4 else xd)
+    for off in first_group + second_group:
+        either_way(off, w1[off][1].start, w1[off][2].start)
     for pair in x_fwd:
         either(pair[0], lambda c: c.wait_recv(), pair[1], pair[2])
     order = (y_far, y_mate, y_next, y)
@@ -490,10 +531,20 @@
         lanes = slice(128 * head, 128 * (head + 1))
         dke[head, n, 0] = (acc[0:512, lanes] * factor).astype(BF)
         dke[head, n, 1] = (acc[1024:1536, lanes] * factor).astype(BF)
-        edges[head] += [
-            go(dke.at[head, n, 0], dk_r.at[head, n, 1], cd),
-            go(dke.at[head, n, 1], dk_r.at[head, n, 0], cu),
-        ]
+        pair = (
+            net.make(dke.at[head, n, 0], dk_r.at[head, n, 1], cd),
+            net.make(dke.at[head, n, 1], dk_r.at[head, n, 0], cu),
+        )
+        edges[head] += pair
+        if (head, n) == (0, 0):
+            pair[0].start()
+            pair[1].start()
+        else:
+            pl.when(z != 0)(pair[0].start)
+            pl.when(z != NZ - 1)(pair[1].start)
+
+    def leave_row(head, n, row):
+        pl.when(z == row)(edges[head][2 * n + (row != 0)].start)
 
     def leave_q(head):
         lanes = slice(128 * head, 128 * (head + 1))
@@ -502,8 +553,8 @@
         locals_out.append(here_now(dq.at[mine, lanes], o_dq.at[:, cols]))
 
     def sum_x(off):
-        w2u[off].wait_recv()
-        w2d[off].wait_recv()
+        w2u[off][0].wait_recv()
+        w2d[off][0].wait_recv()
         add(wg_x.at[off], piece(x, off), wg_r2.at[0, off], wg_r2.at[1, off])
 
     def z_step(s, up, dn):
@@ -541,8 +592,18 @@
         )
         for d in range(1, NX)
     ]
-    d0_z = [net.make(d0_s, d0_zr.at[d - 1], device(x, 0, y, core)) for d in range(1, NZ)]
-    d0_o = [net.make(d0_t, d0_q.at[d - 1], device(0, z, y, core)) for d in range(1, NX)]
+    z_send = net.numbers()
+    net.n_recv += NZ - 2
+    d0_z = [
+        net.make(d0_s, d0_zr.at[d - 1], device(x, 0, y, core), (z_send[0], z_send[1] + d - 1))
+        for d in range(1, NZ)
+    ]
+    o_send = net.numbers()
+    d0_o = [
+        net.make(d0_t, d0_q.at[d - 1], device(0, z, y, core), (o_send[0], o_send[1] + d - 1))
+        for d in range(1, NX)
+    ]
+    net.n_recv += NX - 2
 
     sum_x(4)
     add(wz_s.at[0, 0, 0:128, :], wg_x.at[4, 0:128, :])
@@ -554,6 +615,8 @@
     sum_x(3)
     sum_x(5)
     up, dn = z_step(2, up, dn)
+    leave_row(0, 1, 0)
+    leave_row(0, 1, NZ - 1)
     leave(1, 0)
 
     a1n.wait_recv()
@@ -569,15 +632,7 @@
     sum_x(6)
     up, dn = z_step(3, up, dn)
     leave(1, 1)
-
-    for c in d0_x:
-        c.wait_recv()
-    add(d0_s, d0_b.at[quarter, :], *[d0_xr.at[d] for d in range(3)])
-    for d in range(1, NZ):
-
-        @pl.when(z == d)
-        def _():
-            d0_z[d - 1].start()
+    leave_row(1, 0, 0)
 
     kv_mate, kv_here = [[], []], [[], []]
 
@@ -607,10 +662,22 @@
         for c in kv_here[head]:
             pl.when(cell != 0)(c.start)
 
-    finish(0)
+    for c in d0_x:
+        c.wait_recv()
+    add(d0_s, d0_b.at[quarter, :], *[d0_xr.at[d] for d in range(3)])
+    for d in range(1, NZ):
+
+        @pl.when(z == d)
+        def _():
+            d0_z[d - 1].start()
+
+    leave_row(1, 0, NZ - 1)
     sum_x(1)
     sum_x(7)
     up, dn = z_step(4, up, dn)
+    leave_row(1, 1, 0)
+    leave_row(1, 1, NZ - 1)
+    finish(0)
 
     @pl.when(z == 0)
     def _():
@@ -623,14 +690,23 @@
             def _():
                 d0_o[d - 1].start()
 
+    sum_x(0)
+    w_last = net.make(w_out.at[rows(64 * (1 - ylo), 64), :], o_wg.at[:, mine], mate)
+    w_here = here(w_out.at[rows(64 * ylo, 64), :], o_wg.at[:, mine])
+    locals_out.append(w_here)
+
+    def last_sum():
+        up.wait_recv()
+        dn.wait_recv()
+        add(wg_x.at[0], wg_x.at[0], wz_r.at[0, 3], wz_r.at[1, 3])
+        w_out[...] = wg_x[0].T
+        w_last.start()
+        w_here.start()
+
+    edge_row = (z == 0) | (z == NZ - 1)
+    pl.when(edge_row)(last_sum)
     finish(1)
-    sum_x(0)
-    up.wait_recv()
-    dn.wait_recv()
-    add(wg_x.at[0], wg_x.at[0], wz_r.at[0, 3], wz_r.at[1, 3])
-    w_out[...] = wg_x[0].T
-    w_last = go(w_out.at[rows(64 * (1 - ylo), 64), :], o_wg.at[:, mine], mate)
-    locals_out.append(here_now(w_out.at[rows(64 * ylo, 64), :], o_wg.at[:, mine]))
+    pl.when(jnp.logical_not(edge_row))(last_sum)
 
     @pl.when(cell == 0)
     def _():
@@ -659,10 +735,16 @@
         c.wait_recv()
     for c in locals_out + kv_here[0] + kv_here[1]:
         c.wait()
-    for c in ends + kv_mate[0] + kv_mate[1]:
+    net.drain()
+    assert (net.n_send, net.n_recv, n_local[0]) == COUNTS, (net.n_send, net.n_recv, n_local)
+    for c in kv_mate[0] + kv_mate[1] + edges[0] + edges[1] + [w_last]:
         c.wait_send()
     for pair in x_fwd:
         either(pair[0], lambda c: c.wait_send(), pair[1], pair[2])
+    for off in first_group + second_group:
+        either_way(off, w1[off][1].wait_send, w1[off][2].wait_send)
+        w2u[off][0].wait_send()
+        w2d[off][0].wait_send()
 
     @pl.when(cell == 0)
     def _():
@@ -760,9 +842,9 @@
         b(3, 64, 256),
         f(2, 512, 256),
         b(2, 512, 256),
-        pltpu.SemaphoreType.DMA((N_COPIES,)),
-        pltpu.SemaphoreType.DMA((N_COPIES,)),
-        pltpu.SemaphoreType.DMA((24,)),
+        pltpu.SemaphoreType.DMA((N_SEND,)),
+        pltpu.SemaphoreType.DMA((N_RECV,)),
+        pltpu.SemaphoreType.DMA((N_LOCAL,)),
     ]
     outs = pl.pallas_call(
         layer_kernel,

time: 93 us -> 89 us (0.957)
  Pallas kernels: 90.5 us -> 86.6 us
    pallas_call x1, Pallas kernels: 88.3 us -> 84.4 us  [local(): pl.pallas_call(layer_kernel, out_shape=results, in_specs=anywhere(6), out...]
where the time goes in v4:
time: 89 us; the launch traced here: 87.2 us
  Pallas kernels  86.6 us (97%)
    pallas_call x1, Pallas kernels, local(): pl.pallas_call(layer_kernel, out_shape=results, in_specs=anywhere(6), out...  84.4 us
    pallas_call x1, Pallas kernels, local(): pl.pallas_call(hand_over_kernel, out_shape=results, in_specs=anywhere(5),...  2.22 us

profile of v4, /device:TPU:16, one launch (start us, length us, event | category | flops | bytes accessed | tf_op | source)
XLA Modules:
  0.0 87.2 jit_solution(15597760634850791592)
XLA Ops:
  0.6 84.4 %layer.1 = (bf16[256,1024]{1,0:T(8,128)(2,1)}, bf16[256,512]{1,0:T(8,128)(2,1)}, bf16[256,512]{1,0:T(8,128)(2,1)}, bf16[256,512]{1,0:T(8,128)(2,1)}, f32[64,512]{1,0:T(8,128)}) custom-call(bf16[256,512]{1,0:T(8,128)(2,1)} %q.1, bf16[256,512]{1,0:T(8,128)(2,1)} %k.1, bf16[256,512]{1,0:T(8,128)(2,1)} %v.1, bf16[64,512]{1,0:T(8,128)(2,1)} %w.1, ...), custom_call_target="tpu_custom_call" | custom-call | tf_op jit(solution)/shard_map/layer/pallas_call | solution.py:849
  85.0 2.2 %hand_over.1 = (bf16[256,1024]{1,0:T(8,128)(2,1)}, bf16[256,512]{1,0:T(8,128)(2,1)}, bf16[256,512]{1,0:T(8,128)(2,1)}, bf16[256,512]{1,0:T(8,128)(2,1)}, f32[64,512]{1,0:T(8,128)}) custom-call(bf16[256,1024]{1,0:T(8,128)(2,1)} %get-tuple-element.10.refs_0_, bf16[256,512]{1,0:T(8,128)(2,1)} %get-tuple-element.11.refs_1_, ...), custom_call_target="tpu_custom_call" | custom-call | tf_op jit(solution)/shard_map/hand_over/pallas_call | solution.py:860

commit v5 on v4

--- a/solution.py
+++ b/solution.py
@@ -11,8 +11,8 @@
 BF = jnp.bfloat16
 F32 = jnp.float32
 NX, NZ, NY = 4, 8, 4
-POOL = 40
-COUNTS = N_SEND, N_RECV, N_LOCAL = 106, 150, 16
+POOL = 64
+COUNTS = N_SEND, N_RECV, N_LOCAL = 81, 122, 16
 
 
 def place():
@@ -35,10 +35,17 @@
         self.send, self.recv = send, recv
         self.n_send, self.n_recv, self.live = POOL, 0, []
 
-    def numbers(self):
+    def new_send(self):
         self.n_send += 1
+        return self.n_send - 1
+
+    def new_recv(self):
         self.n_recv += 1
-        return self.n_send - 1, self.n_recv - 1
+        return self.n_recv - 1
+
+    def numbers(self, k_send=None, k_recv=None):
+        k_send = self.new_send() if k_send is None else k_send
+        return k_send, self.new_recv() if k_recv is None else k_recv
 
     def make(self, src, dst, target, numbers=None):
         k_send, k_recv = numbers or self.numbers()
@@ -51,13 +58,12 @@
             device_id_type=pl.DeviceIdType.MESH,
         )
 
-    def start(self, src, dst, target):
+    def start(self, src, dst, target, k_recv=None):
         k_send = len(self.live)
         if k_send == POOL:
             k_send, oldest = self.live.pop(0)
             oldest.wait_send()
-        self.n_recv += 1
-        c = self.make(src, dst, target, (k_send, self.n_recv - 1))
+        c = self.make(src, dst, target, self.numbers(k_send, k_recv))
         c.start()
         self.live.append((k_send, c))
         return c
@@ -137,8 +143,15 @@
     hi_mine, hi_other = rows(1024 + 256 * ylo, 256), rows(1024 + 256 * (1 - ylo), 256)
     n_local = [0]
 
-    def go(src, dst, target):
-        return net.start(src, dst, target)
+    def go(src, dst, target, k_recv=None):
+        return net.start(src, dst, target, k_recv)
+
+    def total_of(ref, k_recv=None, k_send=None):
+        return net.make(ref, ref, mate, (k_send or 0, k_recv or 0))
+
+    kv_send, edge_send, w1_send, w2_send, fwd_send, b_send = (net.new_send() for _ in range(6))
+    k_halo, v_halo, d0x_recv, d0z_recv, d0o_recv = (net.new_recv() for _ in range(5))
+    edge_recv = [[net.new_recv() for _ in range(2)] for _ in range(2)]
 
     def here(src, dst):
         c = pltpu.make_async_copy(src, dst, lsem.at[n_local[0]])
@@ -176,7 +189,12 @@
         for d in range(1, NX)
     ]
     b_along_z = [
-        net.make(b0.at[quarter, :], b0.at[quarter, :], device(x, (z + d) % NZ, y, core))
+        net.make(
+            b0.at[quarter, :],
+            b0.at[quarter, :],
+            device(x, (z + d) % NZ, y, core),
+            net.numbers(b_send),
+        )
         for d in range(1, NZ)
     ]
 
@@ -199,8 +217,8 @@
     own_half, mate_half = rows(64 * ylo, 64), rows(64 * (1 - ylo), 64)
     first = [go(w.at[:, mine], wf.at[x, z, own_half, :], t) for t in (zu, zd, xu, xd)]
     halo = [
-        go(k.at[:, mine], kb.at[lo_mine, :], cu),
-        go(k.at[:, mine], kb.at[hi_mine, :], cd),
+        go(k.at[:, mine], kb.at[lo_mine, :], cu, k_halo),
+        go(k.at[:, mine], kb.at[hi_mine, :], cd, k_halo),
     ]
     w_mate.wait_recv()
     w_loc.wait()
@@ -231,7 +249,7 @@
             first[3].wait_recv()
         x_plus[off].wait_recv()
         x_minus[off].wait_recv()
-        ks = net.numbers()
+        ks = net.numbers(fwd_send)
         pair = (
             goes_up(off in (0, 6, 2, 4)),
             net.make(wf.at[x_dn, zz], wf.at[x_dn, zz], xu, ks),
@@ -294,15 +312,15 @@
             b_along_z[n].start()
 
     halo += [
-        go(v.at[:, mine], vb.at[lo_mine, :], cu),
-        go(v.at[:, mine], vb.at[hi_mine, :], cd),
+        go(v.at[:, mine], vb.at[lo_mine, :], cu, v_halo),
+        go(v.at[:, mine], vb.at[hi_mine, :], cd, v_halo),
     ]
     k_mate.wait_recv()
     k_loc.wait()
     up, dn = ring_step(2, up, dn)
     halo += [
-        go(kb.at[band_other, :], kb.at[lo_other, :], cu),
-        go(kb.at[band_other, :], kb.at[hi_other, :], cd),
+        go(kb.at[band_other, :], kb.at[lo_other, :], cu, k_halo),
+        go(kb.at[band_other, :], kb.at[hi_other, :], cd, k_halo),
     ]
     pass_x(0)
     for d in range(1, NZ):
@@ -329,8 +347,8 @@
     v_loc.wait()
     up, dn = ring_step(3, up, dn)
     halo += [
-        go(vb.at[band_other, :], vb.at[lo_other, :], cu),
-        go(vb.at[band_other, :], vb.at[hi_other, :], cd),
+        go(vb.at[band_other, :], vb.at[lo_other, :], cu, v_halo),
+        go(vb.at[band_other, :], vb.at[hi_other, :], cd, v_halo),
     ]
     from_mate = ogf.at[y_mate % 2, (y_mate // 2) * 2 + core]
     from_next = ogf.at[y_next % 2, (y_next // 2) * 2 + core]
@@ -355,8 +373,8 @@
         for d in range(1, NX):
             b_along_x[d - 1].wait_recv()
 
-    for c in halo:
-        c.wait_recv()
+    total_of(kb.at[0:1024, :], k_halo).wait_recv()
+    total_of(vb.at[0:1024, :], v_halo).wait_recv()
 
     def window(n):
         i, head = n % 4, n // 4
@@ -419,14 +437,16 @@
         part = dot(mixed[rows(256 * (t % 2), 256), :], wf[hh].reshape(1024, 256), NT)
         at[t % 2, hh] = part.astype(BF)
 
-    w1, w2u, w2d = {}, {}, {}
+    w1, w2u, w2d, w2_recv = {}, {}, {}, {}
 
     def piece(xx, off):
         return wg.at[xx, (z + off) % NZ]
 
     first_group, second_group = (4, 3, 5, 2), (6, 1, 7, 0)
     for off in first_group + second_group:
-        ks, ku, kd = net.numbers(), net.numbers(), net.numbers()
+        ks = net.numbers(w1_send)
+        ku = kd = net.numbers(w2_send)
+        w2_recv[off] = ku[1]
         w1[off] = (
             off >= 4 if off in first_group else goes_up(off >= 4),
             net.make(piece(x_far, off), wg_r1.at[off], xu, ks),
@@ -464,47 +484,6 @@
             w2d[off][1].start()
 
         either_way(off, up_way, down_way)
-
-    weight_part(x_far)
-    for off in first_group + second_group:
-        either_way(off, w1[off][1].start, w1[off][2].start)
-    for pair in x_fwd:
-        either(pair[0], lambda c: c.wait_recv(), pair[1], pair[2])
-    order = (y_far, y_mate, y_next, y)
-    cores = []
-    for t in order:
-        attended_part(t, 1 - core)
-        cores.append(go(at.at[t % 2, (t // 2) * 2 + 1 - core], at_core.at[t], twin))
-    weight_part(x_up)
-    weight_part(x_dn)
-    for off in (4, 3, 5, 2):
-        straight(off)
-    for t in order:
-        attended_part(t, core)
-    weight_part(x)
-    for t in range(2):
-        total = jnp.zeros((256, 256), F32)
-        for hh in range(4):
-            total = total + dot(ogf[t, hh], wf[hh].reshape(1024, 256))
-        mgrad[256 * t : 256 * (t + 1), :] = total.astype(BF)
-    dk[...] = jnp.zeros_like(dk)
-    dv[...] = jnp.zeros_like(dv)
-    d0[...] = jnp.zeros_like(d0)
-    for off in (4, 3, 5, 2):
-        relay(off)
-    for off in (6, 1, 7, 0):
-        straight(off)
-
-    for n, t in enumerate(order):
-        cores[n].wait_recv()
-        add(at_sum.at[t], at.at[t % 2, (t // 2) * 2 + core], at_core.at[t])
-        if n == 0:
-            a1n = go(at_sum.at[t, 0:128, :], at_r1.at[0], nxt)
-            a1m = go(at_sum.at[t, 128:256, :], at_r1.at[1], mate)
-        if n == 1:
-            a2m = [go(at_sum.at[t, 128:256, :], at_r2.at[0, 128:256, :], mate)]
-        if n == 2:
-            a2n = [go(at_sum.at[t, 0:128, :], at_r2.at[1, 0:128, :], nxt)]
 
     def backward(n, carry):
         i, head, toks, win, lanes = window(n)
@@ -532,19 +511,12 @@
         dke[head, n, 0] = (acc[0:512, lanes] * factor).astype(BF)
         dke[head, n, 1] = (acc[1024:1536, lanes] * factor).astype(BF)
         pair = (
-            net.make(dke.at[head, n, 0], dk_r.at[head, n, 1], cd),
-            net.make(dke.at[head, n, 1], dk_r.at[head, n, 0], cu),
+            net.make(dke.at[head, n, 0], dk_r.at[head, n, 1], cd, (edge_send, edge_recv[head][n])),
+            net.make(dke.at[head, n, 1], dk_r.at[head, n, 0], cu, (edge_send, edge_recv[head][n])),
         )
         edges[head] += pair
-        if (head, n) == (0, 0):
-            pair[0].start()
-            pair[1].start()
-        else:
-            pl.when(z != 0)(pair[0].start)
-            pl.when(z != NZ - 1)(pair[1].start)
-
-    def leave_row(head, n, row):
-        pl.when(z == row)(edges[head][2 * n + (row != 0)].start)
+        pair[0].start()
+        pair[1].start()
 
     def leave_q(head):
         lanes = slice(128 * head, 128 * (head + 1))
@@ -553,8 +525,7 @@
         locals_out.append(here_now(dq.at[mine, lanes], o_dq.at[:, cols]))
 
     def sum_x(off):
-        w2u[off][0].wait_recv()
-        w2d[off][0].wait_recv()
+        total_of(wg_r2.at[:, off], w2_recv[off]).wait_recv()
         add(wg_x.at[off], piece(x, off), wg_r2.at[0, off], wg_r2.at[1, off])
 
     def z_step(s, up, dn):
@@ -575,12 +546,36 @@
         dn = go(wz_s.at[1, s - 1], wz_r.at[1, s - 1], zd)
         return up, dn
 
+    weight_part(x_far)
+    for off in first_group + second_group:
+        either_way(off, w1[off][1].start, w1[off][2].start)
+    for pair in x_fwd:
+        either(pair[0], lambda c: c.wait_recv(), pair[1], pair[2])
+    order = (y_far, y_mate, y_next, y)
+    cores = []
+    for t in order:
+        attended_part(t, 1 - core)
+        cores.append(go(at.at[t % 2, (t // 2) * 2 + 1 - core], at_core.at[t], twin))
+    weight_part(x_up)
+    weight_part(x_dn)
+    for off in first_group:
+        straight(off)
+    for t in range(2):
+        total = jnp.zeros((256, 256), F32)
+        for hh in range(4):
+            total = total + dot(ogf[t, hh], wf[hh].reshape(1024, 256))
+        mgrad[256 * t : 256 * (t + 1), :] = total.astype(BF)
+    dk[...] = jnp.zeros_like(dk)
+    dv[...] = jnp.zeros_like(dv)
+    d0[...] = jnp.zeros_like(d0)
     lax.fori_loop(0, 4, backward, 0)
-    for off in (6, 1, 7, 0):
+    leave(0, 0)
+    leave(0, 1)
+    leave_q(0)
+    for off in first_group:
         relay(off)
-    leave(0, 0)
-    leave_q(0)
     lax.fori_loop(4, 8, backward, 0)
+    leave(1, 0)
 
     d0_b[0:BLK, :] = (d0[0] * SCALE).astype(BF)
     d0_b[BLK : 2 * BLK, :] = d0[1].astype(BF)
@@ -589,35 +584,48 @@
             d0_b.at[rows(64 * ((x + d) % NX), 64), :],
             d0_xr.at[d - 1],
             device((x + d) % NX, z, y, core),
+            d0x_recv,
         )
         for d in range(1, NX)
     ]
-    z_send = net.numbers()
-    net.n_recv += NZ - 2
+    z_send, o_send = net.new_send(), net.new_send()
     d0_z = [
-        net.make(d0_s, d0_zr.at[d - 1], device(x, 0, y, core), (z_send[0], z_send[1] + d - 1))
+        net.make(d0_s, d0_zr.at[d - 1], device(x, 0, y, core), (z_send, d0z_recv))
         for d in range(1, NZ)
     ]
-    o_send = net.numbers()
     d0_o = [
-        net.make(d0_t, d0_q.at[d - 1], device(0, z, y, core), (o_send[0], o_send[1] + d - 1))
+        net.make(d0_t, d0_q.at[d - 1], device(0, z, y, core), (o_send, d0o_recv))
         for d in range(1, NX)
     ]
-    net.n_recv += NX - 2
+
+    for off in second_group:
+        straight(off)
+    for t in order:
+        attended_part(t, core)
+    weight_part(x)
+    for n, t in enumerate(order):
+        cores[n].wait_recv()
+        add(at_sum.at[t], at.at[t % 2, (t // 2) * 2 + core], at_core.at[t])
+        if n == 0:
+            a1n = go(at_sum.at[t, 0:128, :], at_r1.at[0], nxt)
+            a1m = go(at_sum.at[t, 128:256, :], at_r1.at[1], mate)
+        if n == 1:
+            a2m = [go(at_sum.at[t, 128:256, :], at_r2.at[0, 128:256, :], mate)]
+        if n == 2:
+            a2n = [go(at_sum.at[t, 0:128, :], at_r2.at[1, 0:128, :], nxt)]
+    for off in second_group:
+        relay(off)
 
     sum_x(4)
     add(wz_s.at[0, 0, 0:128, :], wg_x.at[4, 0:128, :])
     up = go(wz_s.at[0, 0, 0:128, :], wz_r.at[0, 0, 0:128, :], zu)
     add(wz_s.at[1, 0, 128:256, :], wg_x.at[4, 128:256, :])
     dn = go(wz_s.at[1, 0, 128:256, :], wz_r.at[1, 0, 128:256, :], zd)
-    leave(0, 1)
     leave_q(1)
     sum_x(3)
     sum_x(5)
     up, dn = z_step(2, up, dn)
-    leave_row(0, 1, 0)
-    leave_row(0, 1, NZ - 1)
-    leave(1, 0)
+    leave(1, 1)
 
     a1n.wait_recv()
     to_mate = at_core.at[0, 0:128, :]
@@ -631,39 +639,34 @@
     sum_x(2)
     sum_x(6)
     up, dn = z_step(3, up, dn)
-    leave(1, 1)
-    leave_row(1, 0, 0)
 
     kv_mate, kv_here = [[], []], [[], []]
 
-    def finish(head):
-        for c in edges[head]:
-            c.wait_recv()
+    def finish(head, n):
+        total_of(dk_r.at[head, n], edge_recv[head][n]).wait_recv()
+        acc, factor = ((dk, SCALE), (dv, 1.0))[n]
+        out = (o_dk, o_dv)[n]
         lanes = slice(128 * head, 128 * (head + 1))
         cols = rows(256 * ylo + 128 * head, 128)
-        for n, (acc, factor) in enumerate(((dk, SCALE), (dv, 1.0))):
-            dkv_s[n, :, lanes] = (
-                acc[512:1024, lanes] * factor
-                + dk_r[head, n, 0].astype(F32)
-                + dk_r[head, n, 1].astype(F32)
-            )
-            out = (o_dk, o_dv)[n]
-            for r in (0, BLK):
-                src = d_out.at[n, rows(256 * (1 - ylo) + r, BLK), lanes]
-                kv_mate[head].append(net.make(src, out.at[r : r + BLK, cols], mate))
-            kv_here[head].append(here(d_out.at[n, mine, lanes], out.at[:, cols]))
-
-        d_out[:, :, lanes] = dkv_s[:, :, lanes].astype(BF)
-        for m, c in enumerate(kv_mate[head]):
-            if m % 2 == 1:
+        dkv_s[n, :, lanes] = (
+            acc[512:1024, lanes] * factor
+            + dk_r[head, n, 0].astype(F32)
+            + dk_r[head, n, 1].astype(F32)
+        )
+        d_out[n, :, lanes] = dkv_s[n, :, lanes].astype(BF)
+        for r in (0, BLK):
+            src = d_out.at[n, rows(256 * (1 - ylo) + r, BLK), lanes]
+            c = net.make(src, out.at[r : r + BLK, cols], mate, net.numbers(kv_send))
+            kv_mate[head].append(c)
+            if r == 0:
+                pl.when((cell != 0) | (ylo == 0))(c.start)
+            else:
                 c.start()
-            else:
-                pl.when((cell != 0) | (ylo == 0))(c.start)
-        for c in kv_here[head]:
-            pl.when(cell != 0)(c.start)
-
-    for c in d0_x:
-        c.wait_recv()
+        c = here(d_out.at[n, mine, lanes], out.at[:, cols])
+        kv_here[head].append(c)
+        pl.when(cell != 0)(c.start)
+
+    total_of(d0_xr, d0x_recv).wait_recv()
     add(d0_s, d0_b.at[quarter, :], *[d0_xr.at[d] for d in range(3)])
     for d in range(1, NZ):
 
@@ -671,18 +674,15 @@
         def _():
             d0_z[d - 1].start()
 
-    leave_row(1, 0, NZ - 1)
     sum_x(1)
     sum_x(7)
     up, dn = z_step(4, up, dn)
-    leave_row(1, 1, 0)
-    leave_row(1, 1, NZ - 1)
-    finish(0)
+    finish(0, 0)
+    finish(0, 1)
 
     @pl.when(z == 0)
     def _():
-        for c in d0_z:
-            c.wait_recv()
+        total_of(d0_zr, d0z_recv).wait_recv()
         add(d0_t, d0_s, *[d0_zr.at[d] for d in range(NZ - 1)])
         for d in range(1, NX):
 
@@ -705,13 +705,15 @@
 
     edge_row = (z == 0) | (z == NZ - 1)
     pl.when(edge_row)(last_sum)
-    finish(1)
+    finish(1, 0)
+
+    finish(1, 1)
+
     pl.when(jnp.logical_not(edge_row))(last_sum)
 
     @pl.when(cell == 0)
     def _():
-        for c in d0_o:
-            c.wait_recv()
+        total_of(d0_q, d0o_recv).wait_recv()
         for m in range(4):
             part = d0_t[...] if m == 0 else d0_q[m - 1]
             dkv_s[m // 2, 64 * (m % 2) : 64 * (m % 2) + 64, :] += part.astype(F32)
@@ -737,14 +739,10 @@
         c.wait()
     net.drain()
     assert (net.n_send, net.n_recv, n_local[0]) == COUNTS, (net.n_send, net.n_recv, n_local)
-    for c in kv_mate[0] + kv_mate[1] + edges[0] + edges[1] + [w_last]:
-        c.wait_send()
-    for pair in x_fwd:
-        either(pair[0], lambda c: c.wait_send(), pair[1], pair[2])
-    for off in first_group + second_group:
-        either_way(off, w1[off][1].wait_send, w1[off][2].wait_send)
-        w2u[off][0].wait_send()
-        w2d[off][0].wait_send()
+    w_last.wait_send()
+    total_of(d_out.at[:, 0:256, :], k_send=kv_send).wait_send()
+    for sent, k_send in ((dke, edge_send), (wg_r1, w1_send), (wg_r2, w2_send), (wf.at[0], fwd_send)):
+        total_of(sent, k_send=k_send).wait_send()
 
     @pl.when(cell == 0)
     def _():
@@ -760,8 +758,7 @@
 
     @pl.when(z == 0)
     def _():
-        for c in b_along_z:
-            c.wait_send()
+        total_of(d0_zr, k_send=b_send).wait_send()
 
         for d in range(1, NX):
 

time: 89 us -> 85.6 us (0.962); the launches traced: 87.2 us -> 85.5 us
  Pallas kernels: 86.6 us -> 84.8 us
    pallas_call x1, Pallas kernels: 84.4 us -> 82.6 us  [local(): pl.pallas_call(layer_kernel, out_shape=results, in_specs=anywhere(6), out...]
where the time goes in v5:
time: 85.6 us; the launch traced here: 85.5 us
  Pallas kernels  84.8 us (99%)
    pallas_call x1, Pallas kernels, local(): pl.pallas_call(layer_kernel, out_shape=results, in_specs=anywhere(6), out...  82.6 us
    pallas_call x1, Pallas kernels, local(): pl.pallas_call(hand_over_kernel, out_shape=results, in_specs=anywhere(5),...  2.22 us

profile of v5, /device:TPU:16, one launch (start us, length us, event | category | flops | bytes accessed | tf_op | source)
XLA Modules:
  0.0 85.5 jit_solution(15257896564232491479)
XLA Ops:
  0.6 82.6 %layer.1 = (bf16[256,1024]{1,0:T(8,128)(2,1)}, bf16[256,512]{1,0:T(8,128)(2,1)}, bf16[256,512]{1,0:T(8,128)(2,1)}, bf16[256,512]{1,0:T(8,128)(2,1)}, f32[64,512]{1,0:T(8,128)}) custom-call(bf16[256,512]{1,0:T(8,128)(2,1)} %q.1, bf16[256,512]{1,0:T(8,128)(2,1)} %k.1, bf16[256,512]{1,0:T(8,128)(2,1)} %v.1, bf16[64,512]{1,0:T(8,128)(2,1)} %w.1, ...), custom_call_target="tpu_custom_call" | custom-call | tf_op jit(solution)/shard_map/layer/pallas_call | solution.py:846
  83.2 2.2 %hand_over.1 = (bf16[256,1024]{1,0:T(8,128)(2,1)}, bf16[256,512]{1,0:T(8,128)(2,1)}, bf16[256,512]{1,0:T(8,128)(2,1)}, bf16[256,512]{1,0:T(8,128)(2,1)}, f32[64,512]{1,0:T(8,128)}) custom-call(bf16[256,1024]{1,0:T(8,128)(2,1)} %get-tuple-element.10.refs_0_, bf16[256,512]{1,0:T(8,128)(2,1)} %get-tuple-element.11.refs_1_, ...), custom_call_target="tpu_custom_call" | custom-call | tf_op jit(solution)/shard_map/hand_over/pallas_call | solution.py:857

commit v6 on v5

--- a/solution.py
+++ b/solution.py
@@ -448,7 +448,7 @@
         ku = kd = net.numbers(w2_send)
         w2_recv[off] = ku[1]
         w1[off] = (
-            off >= 4 if off in first_group else goes_up(off >= 4),
+            goes_up(off >= 4),
             net.make(piece(x_far, off), wg_r1.at[off], xu, ks),
             net.make(piece(x_far, off), wg_r1.at[off], xd, ks),
         )
@@ -462,12 +462,8 @@
         )
 
     def either_way(off, up_way, down_way):
-        is_up = w1[off][0]
-        if isinstance(is_up, bool):
-            (up_way if is_up else down_way)()
-        else:
-            pl.when(is_up)(up_way)
-            pl.when(jnp.logical_not(is_up))(down_way)
+        pl.when(w1[off][0])(up_way)
+        pl.when(jnp.logical_not(w1[off][0]))(down_way)
 
     def straight(off):
         either_way(off, w2d[off][0].start, w2u[off][0].start)
@@ -674,12 +670,11 @@
         def _():
             d0_z[d - 1].start()
 
+    finish(0, 0)
+    finish(0, 1)
     sum_x(1)
     sum_x(7)
     up, dn = z_step(4, up, dn)
-    finish(0, 0)
-    finish(0, 1)
-
     @pl.when(z == 0)
     def _():
         total_of(d0_zr, d0z_recv).wait_recv()

time: 85.6 us -> 84.7 us (0.989)
  Pallas kernels: 84.8 us -> 83.4 us
    pallas_call x1, Pallas kernels: 82.6 us -> 81.2 us  [local(): pl.pallas_call(layer_kernel, out_shape=results, in_specs=anywhere(6), out...]
where the time goes in v6:
time: 84.7 us; the launch traced here: 84 us
  Pallas kernels  83.4 us (98%)
    pallas_call x1, Pallas kernels, local(): pl.pallas_call(layer_kernel, out_shape=results, in_specs=anywhere(6), out...  81.2 us
    pallas_call x1, Pallas kernels, local(): pl.pallas_call(hand_over_kernel, out_shape=results, in_specs=anywhere(5),...  2.22 us

profile of v6, /device:TPU:16, one launch (start us, length us, event | category | flops | bytes accessed | tf_op | source)
XLA Modules:
  0.0 84.0 jit_solution(1223439186451142615)
XLA Ops:
  0.6 81.2 %layer.1 = (bf16[256,1024]{1,0:T(8,128)(2,1)}, bf16[256,512]{1,0:T(8,128)(2,1)}, bf16[256,512]{1,0:T(8,128)(2,1)}, bf16[256,512]{1,0:T(8,128)(2,1)}, f32[64,512]{1,0:T(8,128)}) custom-call(bf16[256,512]{1,0:T(8,128)(2,1)} %q.1, bf16[256,512]{1,0:T(8,128)(2,1)} %k.1, bf16[256,512]{1,0:T(8,128)(2,1)} %v.1, bf16[64,512]{1,0:T(8,128)(2,1)} %w.1, ...), custom_call_target="tpu_custom_call" | custom-call | tf_op jit(solution)/shard_map/layer/pallas_call | solution.py:841
  81.8 2.2 %hand_over.1 = (bf16[256,1024]{1,0:T(8,128)(2,1)}, bf16[256,512]{1,0:T(8,128)(2,1)}, bf16[256,512]{1,0:T(8,128)(2,1)}, bf16[256,512]{1,0:T(8,128)(2,1)}, f32[64,512]{1,0:T(8,128)}) custom-call(bf16[256,1024]{1,0:T(8,128)(2,1)} %get-tuple-element.10.refs_0_, bf16[256,512]{1,0:T(8,128)(2,1)} %get-tuple-element.11.refs_1_, ...), custom_call_target="tpu_custom_call" | custom-call | tf_op jit(solution)/shard_map/hand_over/pallas_call | solution.py:852

commit v7 on v6

--- a/solution.py
+++ b/solution.py
@@ -207,7 +207,7 @@
     k_mate = go(k.at[:, other], kb.at[band_mine, :], mate)
     v_mate = go(v.at[:, other], vb.at[band_mine, :], mate)
     og_next = go(og, ogf.at[ylo, h], nxt)
-    half, cut = 160, 208
+    half, cut = 176, 208
     og_here = ogf.at[ylo, h]
     og_mate = [go(og.at[0:half, :], og_here.at[0:half, :], mate)]
     q_mate = go(q.at[:, other], q2.at[mine, :], mate)

time: 84.7 us -> 84.7 us (level)
  no operation moved by 1% of the time
where the time goes in v7:
time: 84.7 us; the launch traced here: 84.2 us
  Pallas kernels  83.5 us (99%)
    pallas_call x1, Pallas kernels, local(): pl.pallas_call(layer_kernel, out_shape=results, in_specs=anywhere(6), out...  81.3 us
    pallas_call x1, Pallas kernels, local(): pl.pallas_call(hand_over_kernel, out_shape=results, in_specs=anywhere(5),...  2.22 us

profile of v7, /device:TPU:16, one launch (start us, length us, event | category | flops | bytes accessed | tf_op | source)
XLA Modules:
  0.0 84.2 jit_solution(13841423180975879614)
XLA Ops:
  0.6 81.3 %layer.1 = (bf16[256,1024]{1,0:T(8,128)(2,1)}, bf16[256,512]{1,0:T(8,128)(2,1)}, bf16[256,512]{1,0:T(8,128)(2,1)}, bf16[256,512]{1,0:T(8,128)(2,1)}, f32[64,512]{1,0:T(8,128)}) custom-call(bf16[256,512]{1,0:T(8,128)(2,1)} %q.1, bf16[256,512]{1,0:T(8,128)(2,1)} %k.1, bf16[256,512]{1,0:T(8,128)(2,1)} %v.1, bf16[64,512]{1,0:T(8,128)(2,1)} %w.1, ...), custom_call_target="tpu_custom_call" | custom-call | tf_op jit(solution)/shard_map/layer/pallas_call | solution.py:841
  81.9 2.2 %hand_over.1 = (bf16[256,1024]{1,0:T(8,128)(2,1)}, bf16[256,512]{1,0:T(8,128)(2,1)}, bf16[256,512]{1,0:T(8,128)(2,1)}, bf16[256,512]{1,0:T(8,128)(2,1)}, f32[64,512]{1,0:T(8,128)}) custom-call(bf16[256,1024]{1,0:T(8,128)(2,1)} %get-tuple-element.10.refs_0_, bf16[256,512]{1,0:T(8,128)(2,1)} %get-tuple-element.11.refs_1_, ...), custom_call_target="tpu_custom_call" | custom-call | tf_op jit(solution)/shard_map/hand_over/pallas_call | solution.py:852
